TPU v7x, 256 devices: a whole 4x4x8 slice. The times are simulated.
256 devices in a mesh: inst: 8 (over y, x_lo), scen: 32 (over x_hi, z, core).
Axes of the slice: x: 4 (x_hi: 2, x_lo: 2; x = x_hi * 2 + x_lo), y: 4, z: 8, core: 2. Of those that a mesh axis runs over, the one named last changes fastest.
Arguments:
- positions: int32 [512, 16384], P(None, 'inst'), may hold values from -50 to 50
- holding_block_grid: int32 [8, 128], P(None, 'inst'), may hold values 0 or 1
- risk: float32 [16384, 32768], P('inst', 'scen'), may hold values from -64 to 64
Outputs:
- margin: float32 [512], P('inst')
- gradient: float32 [512, 16384], P('scen', 'inst')
All inputs are finite; a program needn't handle non-finite values. No bound on the sum of `holding_block_grid` on one device may be relied on, other than what follows from the above.
Results may differ from a plain program's by a relative error of at most 0.0003.
Values sent between devices are 32-bit elements; how exact they have to be, the bound alone decides.
No kernel may reach another device: no remote copies, remote signals or barrier semaphores. Data moves between devices by JAX's collectives and lax.ppermute only.
A program may use at most 64 MiB of HBM per device.

v0:
```python
import math

import jax
import jax.numpy as jnp
from jax import lax
from jax.sharding import Mesh
from jax.sharding import PartitionSpec as P

INSTRUMENT_TOTAL = 16384
ABLK = 64
IBLK = 128
SCEN = ("scen_0", "scen_1", "scen_2")


def in_blocks(array, dim, peers):
    shape = array.shape
    blocks = array.reshape(*shape[:dim], peers, shape[dim] // peers, *shape[dim + 1 :])
    return jnp.moveaxis(blocks, dim, 0)


def sum_at_owner(array, axis, dim):
    peers = lax.axis_size(axis)
    blocks = lax.all_to_all(in_blocks(array, dim, peers), axis, 0, 0, tiled=True)
    return jnp.sum(blocks, axis=0)


def copy_for_each(array, axis):
    peers = lax.axis_size(axis)
    return lax.all_to_all(
        jnp.broadcast_to(array[None], (peers, *array.shape)), axis, 0, 0, tiled=True
    )


def all_in_one(array, axis):
    leaves = jax.tree.leaves(array)
    order = sorted(range(len(leaves)), key=lambda k: -leaves[k].size)
    width = (1, *leaves[order[0]].shape)[-1]
    lines = [
        jnp.pad(leaves[k].reshape(-1), (0, -leaves[k].size % width)).reshape(-1, width)
        for k in order
    ]
    both, at, found = (copy_for_each(jnp.concatenate(lines), axis), 0, {})
    for k, line in zip(order, lines):
        section = both[:, at : at + len(line)].reshape(len(both), -1)
        found[k] = section[:, : leaves[k].size].reshape(-1, *leaves[k].shape)
        at += len(line)
    numbers = iter(range(len(leaves)))
    return jax.tree.map(lambda _: found[next(numbers)], array)


def folded_in_pairs(pieces, combine):
    while len(jax.tree.leaves(pieces)[0]) > 1:
        pieces = jax.vmap(combine)(
            *(jax.tree.map(lambda part: part[side::2], pieces) for side in (0, 1))
        )
    return jax.tree.map(lambda part: part[0], pieces)


def merged(array, axis, combine):
    pieces = all_in_one(array, axis)
    return folded_in_pairs(pieces, combine)


def laid_out(blocks, dim):
    blocks = jnp.moveaxis(blocks, 0, dim)
    shape = blocks.shape
    return blocks.reshape(*shape[:dim], shape[dim] * shape[dim + 1], *shape[dim + 2 :])


def collect(array, axis, dim):
    blocks = copy_for_each(array, axis)
    return laid_out(blocks, dim)


def summed_rows(array, axes, dim):
    far, near = axes
    blocks = in_blocks(array, dim, lax.axis_size(far))
    nearer = sum_at_owner(blocks, near, dim + 1)
    arrived = lax.all_to_all(nearer, far, split_axis=0, concat_axis=0, tiled=True)
    return arrived.sum(axis=0)


def combine_tails(first, second):
    larger = jnp.maximum(first[0], second[0])
    summed = first[1] * jnp.exp(first[0] - larger) + second[1] * jnp.exp(second[0] - larger)
    return (larger, summed)


def body(positions, holding_block_grid, risk):
    accounts = positions.shape[0]
    scenario_number = lax.axis_size(SCEN)
    block_rows = holding_block_grid.shape[0]
    block_cols = holding_block_grid.shape[1]
    live_mask = jnp.broadcast_to(
        holding_block_grid[:, None, :, None], (block_rows, ABLK, block_cols, IBLK)
    ).reshape(accounts, block_cols * IBLK)
    held = (positions * live_mask).astype(jnp.float32)
    softness_level = 8.0 * math.sqrt(INSTRUMENT_TOTAL)
    total_scen = risk.shape[1] * scenario_number
    selected_tail = held
    profit_and_losses = sum_at_owner(
        jnp.dot(
            selected_tail, risk, precision=lax.Precision.HIGHEST, preferred_element_type=jnp.float32
        ),
        "inst",
        0,
    )
    tail_logits = -profit_and_losses / softness_level
    local_peak = jnp.max(tail_logits, axis=1)
    local_total = jnp.sum(jnp.exp(tail_logits - local_peak[:, None]), axis=1)
    peak, total = merged((local_peak, local_total), SCEN, combine_tails)
    shifted = jnp.exp(tail_logits - peak[:, None])
    margin_all = peak + jnp.log(total) - math.log(total_scen)
    weights = shifted / total[:, None]
    weights_all = collect(weights, "inst", 0)
    selected_tail = weights_all
    gradient = summed_rows(
        -jnp.einsum("as,is->ai", selected_tail, risk, precision=lax.Precision.HIGHEST),
        (("scen_0", "scen_1"), "scen_2"),
        0,
    )
    return (margin_all, gradient)


def solution(mesh):
    torus = Mesh(
        mesh.devices.reshape(mesh.shape["inst"], 2, 8, 2), ("inst", "scen_0", "scen_1", "scen_2")
    )
    return jax.shard_map(
        body,
        mesh=torus,
        in_specs=(P(None, "inst"), P(None, "inst"), P("inst", SCEN)),
        out_specs=(P("inst"), P(SCEN, "inst")),
        check_vma=False,
    )
```

profile of v0, /device:TPU:2, one launch (start us, length us, event | category | flops | bytes accessed | tf_op | source)
XLA Modules:
  0.0 190.7 jit_solution(11893998581814290074)
XLA Ops:
  0.6 0.0 copy-start
  0.6 1.2 broadcast_in_dim.6
  1.8 1.0 copy-done
  2.8 18.3 %fusion.1 = f32[512,1024]{1,0:T(8,128)S(1)} fusion(f32[2048,1024]{1,0:T(8,128)} %param.5, s32[512,2048]{1,0:T(8,128)S(1)} %copy-done, s32[64,8,16,128]{3,2,1,0:T(8,128)S(1)} %bitcast.28), kind=kOutput, calls=%fused_computation.2 | convolution fusion | flops 12886999040 | bytes 18874368 | tf_op jit(solution)/shard_map/dot_general | solution.py:102
  21.2 31.5 %all_to_all.25 = f32[8,64,1024]{2,1,0:T(8,128)S(1)} all-to-all(f32[8,64,1024]{2,1,0:T(8,128)S(1)} %bitcast.31), channel_id=1, replica_groups=mesh['inst'=8,'scen_0'=2,'scen_1'=8,'scen_2'=2] {'inst'}, dimensions={0} | all-to-all | bytes 4194304 | tf_op jit(solution)/shard_map/all_to_all | solution.py:23
  52.7 0.1 reduce_sum.36
  52.8 0.1 fusion.4
  52.9 0.2 exponential_reduce_fusion
  53.2 0.1 reshape.68
  53.3 20.1 %all_to_all.26 = f32[32,1,128]{2,1,0:T(1,128)S(1)} all-to-all(f32[32,1,128]{2,1,0:T(1,128)S(1)} %reshape.68), channel_id=1, replica_groups=mesh['inst'=8,'scen_0'=2,'scen_1'=8,'scen_2'=2] {'scen_0','scen_1','scen..., dimensions={0} | all-to-all | bytes 32768 | tf_op jit(solution)/shard_map/all_to_all | solution.py:29
  73.4 0.5 broadcast.27
  73.9 0.7 reduce
  74.6 0.1 reshape.69
  75.1 0.5 add_add_fusion
  75.7 0.1 exponential_divide_fusion
  75.8 0.2 broadcast_in_dim.8
  76.1 30.4 %all_to_all.27 = f32[8,64,1024]{2,1,0:T(8,128)S(1)} all-to-all(f32[8,64,1024]{2,1,0:T(8,128)S(1)} %broadcast_in_dim.8), channel_id=1, replica_groups=mesh['inst'=8,'scen_0'=2,'scen_1'=8,'scen_2'=2] {'inst'}, dimensions={0} | all-to-all | bytes 4194304 | tf_op jit(solution)/shard_map/all_to_all | solution.py:29
  106.5 16.1 %convolution_negate_fusion = f32[512,2048]{1,0:T(8,128)S(1)} fusion(f32[512,1024]{1,0:T(8,128)S(1)} %bitcast.32, f32[2048,1024]{1,0:T(8,128)} %param.5), kind=kOutput, calls=%fused_computation.5 | convolution fusion | flops 12885950464 | bytes 14680064 | tf_op jit(solution)/shard_map/as,is->ai/dot_general | solution.py:118
  122.6 0.3 copy.16
  122.9 8.2 %all_to_all.28 = f32[2,16,16,2048]{3,2,1,0:T(8,128)} all-to-all(f32[2,16,16,2048]{3,2,1,0:T(8,128)S(1)} %bitcast.30), channel_id=1, replica_groups=mesh['inst'=8,'scen_0'=2,'scen_1'=8,'scen_2'=2] {'scen_2'}, dimensions={0} | all-to-all | bytes 8388608 | tf_op jit(solution)/shard_map/all_to_all | solution.py:23
  131.1 2.7 %reduce_sum.38 = f32[16,16,2048]{2,1,0:T(8,128)S(1)} reduce(f32[2,16,16,2048]{3,2,1,0:T(8,128)} %all_to_all.28, f32[]{:T(128)} %constant.4.clone.1), dimensions={0}, to_apply=%region_3.4 | reduce | flops 524288 | bytes 6291460 | tf_op jit(solution)/shard_map/reduce_sum | solution.py:24
  133.8 54.5 %all_to_all.29 = f32[16,16,2048]{2,1,0:T(8,128)} all-to-all(f32[16,16,2048]{2,1,0:T(8,128)S(1)} %reduce_sum.38), channel_id=1, replica_groups=mesh['inst'=8,'scen_0'=2,'scen_1'=8,'scen_2'=2] {'scen_0','scen_1'}, dimensions={0} | all-to-all | bytes 4194304 | tf_op jit(solution)/shard_map/all_to_all | solution.py:79
  188.3 2.4 %reduce_sum.39 = f32[16,2048]{1,0:T(8,128)} reduce(f32[16,16,2048]{2,1,0:T(8,128)} %all_to_all.29, f32[]{:T(128)} %constant.4.clone.1), dimensions={0}, to_apply=%region_4.5 | reduce | flops 491520 | bytes 2228228 | tf_op jit(solution)/shard_map/reduce_sum | solution.py:80
  (23 shorter events, 0.4 us)
Async XLA Ops:
  0.6 2.2 %copy-start = (s32[512,2048]{1,0:T(8,128)S(1)}, s32[512,2048]{1,0:T(8,128)}, u32[]{:S(2)}) copy-start(s32[512,2048]{1,0:T(8,128)} %param.3) | copy-start | bytes 12582916
where the time goes:
time: 192 us; the launch traced here: 191 us
  blocking collectives  145 us (76%)
  matrix products  34.4 us (18%)
  other arithmetic  6.95 us (4%)
  local copies, waits for them, and re-layouts  3.73 us (2%)
    all_to_all x1, blocking collectives, summed_rows(): lax.all_to_all(nearer, far, split_axis=0, concat_axis=0, tiled=True)  54.5 us
    all_to_all x2, blocking collectives, copy_for_each(): lax.all_to_all(jnp.broadcast_to(array[None], (peers, *array.shape)), axis...  50.6 us
    all_to_all x2, blocking collectives, sum_at_owner(): lax.all_to_all(in_blocks(array, dim, peers), axis, 0, 0, tiled=True)  39.7 us
    dot_general x1, matrix products, body(): jnp.dot(selected_tail, risk, precision=lax.Precision.HIGHEST, preferred_e...  18.3 us
    dot_general x1, matrix products, body(): jnp.einsum('as,is->ai', selected_tail, risk, precision=lax.Precision.HIGH...  16.1 us

commit v1 on v0

v1 whole, which is shorter than its diff:
```python
import functools
import math

import jax
import jax.numpy as jnp
from jax import lax
from jax.experimental import pallas as pl
from jax.experimental.pallas import tpu as pltpu
from jax.sharding import Mesh
from jax.sharding import PartitionSpec as P

Y, XL, XH, Z, C = 4, 2, 2, 8, 2
F32, BF16 = jnp.float32, jnp.bfloat16
VMEM = pl.BlockSpec(memory_space=pltpu.VMEM)
HBM = pl.BlockSpec(memory_space=pltpu.HBM)
SB = 256
EXT = 128


def send(x, axis, shift):
    n = lax.axis_size(axis)
    return lax.ppermute(x, axis, [(i, (i + shift) % n) for i in range(n)])


def halves(x):
    high = x.astype(BF16)
    return high, (x - high.astype(F32)).astype(BF16)


def pnl_kernel(
    pos, grid_in, risk, own, oth, b0, b1, b2, b3, posbuf, grid, rbuf, held, high, low, psem, gsem, rsem
):
    y, xl = lax.axis_index("y"), lax.axis_index("xl")
    steps = risk.shape[1] // SB

    def fetch(j, slot):
        return pltpu.make_async_copy(
            risk.at[:, pl.ds(pl.multiple_of(j * SB, SB), SB)], rbuf.at[slot], rsem.at[slot]
        )

    position_copy = pltpu.make_async_copy(pos, posbuf, psem)
    grid_copy = pltpu.make_async_copy(grid_in, grid, gsem)
    grid_copy.start()
    position_copy.start()
    fetch(0, 0).start()
    grid_copy.wait()
    position_copy.wait()
    at = 0
    blocks = [(0, d, e) for e in range(XL) for d in range(Y)]
    blocks += [(1, d, e) for d in range(Y) for e in range(XL)]
    for k, d, e in blocks:
        o = lax.rem(y + d, Y) * 2 + lax.rem(xl + e, XL)
        for pair in range(2):
            row = pl.multiple_of(o * 64 + pair * 32 + k * 8, 8)
            x = jnp.concatenate([posbuf[pl.ds(row, 8), :], posbuf[pl.ds(row + 16, 8), :]], axis=0)
            x = x.astype(F32)
            for i in range(pos.shape[1] // 128):
                live = grid[o, i].astype(F32)
                held[at : at + 16, i * 128 : (i + 1) * 128] = (
                    x[:, i * 128 : (i + 1) * 128] * live
                ).astype(BF16)
            at += 16

    @pl.loop(0, steps)
    def _(j):
        slot = lax.rem(j, 2)
        fetch(j, slot).wait()

        @pl.when(j + 1 < steps)
        def _():
            fetch(j + 1, 1 - slot).start()

        for i in range(0, risk.shape[0], 128):
            high[i : i + 128, :], low[i : i + 128, :] = halves(rbuf[slot, i : i + 128, :])
        cols = pl.ds(pl.multiple_of(j * SB, SB), SB)
        outs = ((0, own), (128, oth), (256, b0), (320, b1), (384, b2), (448, b3))
        acc = jnp.dot(held[...], high[...], preferred_element_type=F32)
        acc += jnp.dot(held[...], low[...], preferred_element_type=F32)
        for first, out in outs:
            out[:, cols] = acc[first : first + out.shape[0]]


def profits(positions, grid, risk):
    rows, n = risk.shape
    accounts = positions.shape[0]
    shape = lambda r: jax.ShapeDtypeStruct((r, n), F32)
    return pl.pallas_call(
        pnl_kernel,
        out_shape=[shape(128), shape(128)] + [shape(64)] * 4,
        in_specs=[HBM, HBM, HBM],
        out_specs=[VMEM] * 6,
        scratch_shapes=[
            pltpu.VMEM((accounts, rows), jnp.int32),
            pltpu.SMEM(grid.shape, jnp.int32),
            pltpu.VMEM((2, rows, SB), F32),
            pltpu.VMEM((accounts, rows), BF16),
            pltpu.VMEM((rows, SB), BF16),
            pltpu.VMEM((rows, SB), BF16),
            pltpu.SemaphoreType.DMA,
            pltpu.SemaphoreType.DMA,
            pltpu.SemaphoreType.DMA((2,)),
        ],
        compiler_params=pltpu.CompilerParams(vmem_limit_bytes=32 << 20),
        cost_estimate=pl.CostEstimate(
            flops=4 * accounts * rows * n, bytes_accessed=12 << 20, transcendentals=0
        ),
    )(*(pltpu.with_memory_space_constraint(a, pltpu.HBM) for a in (positions, grid, risk)))


def grad_kernel(softness, layout, *refs):
    pieces = refs[: len(layout)]
    risk, own, oth, rbuf, tails, stats, high, low, rsem = refs[len(layout) :]
    y, xl, xh, z, c = (lax.axis_index(a) for a in ("y", "xl", "xh", "z", "c"))
    n_inst, n_scen = risk.shape
    steps = n_inst // SB

    def fetch(j, slot):
        return pltpu.make_async_copy(
            risk.at[pl.ds(pl.multiple_of(j * SB, SB), SB), :], rbuf.at[slot], rsem.at[slot]
        )

    fetch(0, 0).start()
    half = XH * Z * 8
    lane = lax.broadcasted_iota(jnp.int32, (8, EXT), 1)
    owned = jnp.zeros((8, EXT), F32)
    for ref, blocks in zip(pieces, layout, strict=True):
        for b, (d, e) in enumerate(blocks):
            o = lax.rem(y + d, Y) * 2 + lax.rem(xl + e, XL)
            other_xh = jnp.where(o // 4 == xh, 0, 1)
            score = ref[b * 32 : b * 32 + 32, :] * (-1.0 / softness)
            peak = jnp.max(score, axis=1, keepdims=True)
            tail = jnp.exp(score - peak)
            total = jnp.sum(tail, axis=1, keepdims=True)
            for t in range(4):
                dz = lax.rem(lax.rem(o, 4) * 2 + t // 2 + Z - z, Z)
                dc = jnp.where(c == t % 2, 0, 1)
                row = pl.multiple_of(((dc * Z + dz) * XH + other_xh) * 8, 8)
                part = slice(t * 8, t * 8 + 8)
                tails[pl.ds(row, 8), :] = tail[part]
                stats[pl.ds(row, 8), :] = jnp.where(lane < 32, peak[part], jnp.where(lane < 64, total[part], 0.0))
                if (d, e) == (0, 0):
                    owned = jnp.where(lane == 64 + t, peak[part], owned)
                    owned = jnp.where(lane == 96 + t, total[part], owned)
    for out, first in ((own, 0), (oth, half)):
        out[:8, n_inst:] = jnp.where(lane < 64, stats[first : first + 8, :], owned)
        out[8:, n_inst:] = stats[first + 8 : first + half, :]
    for i in range(0, 2 * half, 64):
        high[i : i + 64, :], low[i : i + 64, :] = halves(tails[i : i + 64, :])

    def mul(a, b):
        return lax.dot_general(a, b, (((1,), (1,)), ((), ())), preferred_element_type=F32)

    @pl.loop(0, steps)
    def _(j):
        slot = lax.rem(j, 2)
        fetch(j, slot).wait()

        @pl.when(j + 1 < steps)
        def _():
            fetch(j + 1, 1 - slot).start()

        rh, rl = halves(rbuf[slot])
        acc = mul(high[...], rh) + mul(low[...], rh) + mul(high[...], rl)
        cols = pl.ds(pl.multiple_of(j * SB, SB), SB)
        own[:, cols] = acc[:half]
        oth[:, cols] = acc[half:]


def gradients(softness, layout, pieces, risk):
    n_inst, n_scen = risk.shape
    rows = C * XH * Z * 8
    shape = jax.ShapeDtypeStruct((rows // 2, n_inst + EXT), F32)
    return pl.pallas_call(
        functools.partial(grad_kernel, softness, layout),
        out_shape=[shape, shape],
        in_specs=[VMEM] * len(pieces) + [HBM],
        out_specs=[VMEM] * 2,
        scratch_shapes=[
            pltpu.VMEM((2, SB, n_scen), F32),
            pltpu.VMEM((rows, n_scen), F32),
            pltpu.VMEM((rows, EXT), F32),
            pltpu.VMEM((rows, n_scen), BF16),
            pltpu.VMEM((rows, n_scen), BF16),
            pltpu.SemaphoreType.DMA((2,)),
        ],
        compiler_params=pltpu.CompilerParams(vmem_limit_bytes=24 << 20),
        cost_estimate=pl.CostEstimate(
            flops=6 * rows * n_inst * n_scen, bytes_accessed=8 << 20, transcendentals=rows * n_scen
        ),
    )(*pieces, risk)


def merge(parts):
    peaks = [p[:, -EXT : -EXT + 1] for p in parts]
    peak = peaks[0]
    for other in peaks[1:]:
        peak = jnp.maximum(peak, other)
    total = None
    for part, own_peak in zip(parts, peaks, strict=True):
        term = part * jnp.exp(own_peak - peak)
        total = term if total is None else total + term
    lane = lax.broadcasted_iota(jnp.int32, (total.shape[0], EXT), 1)
    return total[:, :-EXT], jnp.where(lane < 32, peak, total[:, -EXT:])


def merge_owned(blocks):
    above = [pltpu.roll(b, 32, 1) for b in blocks]
    largest, peak = blocks[0], above[0]
    for b, a in zip(blocks[1:], above[1:], strict=True):
        largest, peak = jnp.maximum(largest, b), jnp.maximum(peak, a)
    total = sum(b * jnp.exp(a - peak) for b, a in zip(blocks, above, strict=True))
    lane = lax.broadcasted_iota(jnp.int32, (8, EXT), 1)
    return jnp.where(lane < 96, largest, total)


def put(out, rows, parts, owned=None):
    data, stats = merge(parts)
    out[rows, :-EXT] = data
    if owned is not None:
        lane = lax.broadcasted_iota(jnp.int32, stats.shape, 1)
        stats = jnp.where(lane < 64, stats, owned)
    out[rows, -EXT:] = stats


def call(kernel, outs, *args):
    return pl.pallas_call(
        kernel,
        out_shape=[jax.ShapeDtypeStruct(s, F32) for s in outs],
        in_specs=[VMEM] * len(args),
        out_specs=[VMEM] * len(outs),
        compiler_params=pltpu.CompilerParams(vmem_limit_bytes=4 << 20),
        cost_estimate=pl.CostEstimate(
            flops=sum(a.size for a in args), bytes_accessed=8 * sum(a.size for a in args), transcendentals=0
        ),
    )(*args)


LOW, HIGH = slice(0, 8), slice(8, 16)


def core_kernel(own, came, z4a, z4b, z0, z1, z2, z3, z5, z6, z7, acc):
    owned = merge_owned([own[LOW, -EXT:], came[LOW, -EXT:]])
    acc[...] = owned
    for d, out in enumerate((z0, z1, z2, z3, None, z5, z6, z7)):
        for h in range(2):
            rows = slice(d * 16 + h * 8, d * 16 + h * 8 + 8)
            parts = [own[rows, :], came[rows, :]]
            if d == 4:
                put((z4a, z4b)[h], LOW, parts, owned)
            else:
                put(out, (LOW, HIGH)[h], parts)


def first_kernel(z3, up, z5, down, acc, out3, out5, out_acc):
    put(out3, LOW, [z3[LOW, :], up[...]], up[:, -EXT:])
    out3[HIGH, :] = z3[HIGH, :]
    out5[LOW, :-EXT] = z5[LOW, :-EXT]
    lane = lax.broadcasted_iota(jnp.int32, (8, EXT), 1)
    out5[LOW, -EXT:] = jnp.where(lane < 64, z5[LOW, -EXT:], down[:, -EXT:])
    put(out5, HIGH, [z5[HIGH, :], down[...]])
    out_acc[...] = merge_owned([acc[...], up[:, -EXT:], down[:, -EXT:]])


def next_kernel(a, up, b, down, acc, out_a, out_b, out_acc):
    put(out_a, LOW, [a[LOW, :], up[LOW, :]], up[LOW, -EXT:])
    put(out_a, HIGH, [a[HIGH, :], up[HIGH, :]])
    put(out_b, LOW, [b[LOW, :], down[LOW, :]], down[LOW, -EXT:])
    put(out_b, HIGH, [b[HIGH, :], down[HIGH, :]])
    out_acc[...] = merge_owned([acc[...], up[LOW, -EXT:], down[LOW, -EXT:]])


def last_kernel(a, up, down, acc, out_own, out_oth):
    owned = merge_owned([acc[...], up[LOW, -EXT:]])
    for h, out in ((LOW, out_own), (HIGH, out_oth)):
        put(out, LOW, [a[h, :], up[h, :], down[h, :]], owned)


def end_kernel(scenarios, own0, came0, own1, came1, out, margin):
    for h, parts in ((LOW, (own0, came0)), (HIGH, (own1, came1))):
        data, stats = merge([p[...] for p in parts])
        out[h, :] = -data / stats[:, 32:33]
        owned = merge_owned([p[:, -EXT:] for p in parts])
        margin[h, :] = pltpu.roll(owned, 32, 1) + jnp.log(owned) - math.log(scenarios)


def body(positions, grid, risk):
    accounts, n_inst = positions.shape
    n_scen = risk.shape[1]
    softness = 8.0 * math.sqrt(n_inst * Y * XL)
    scenarios = n_scen * XH * Z * C

    own, oth, b0, b1, b2, b3 = profits(positions, grid, risk)
    x0 = send(oth, "xl", 1)
    r1, r3, r2 = send(b1, "y", 1), send(b3, "y", -1), send(b2, "y", 2)
    near = [own[d * 32 : d * 32 + 32] + x0[d * 32 : d * 32 + 32] for d in range(Y)]
    pair = b0 + r1 + r3 + r2
    q1, q3, q2 = send(near[1], "y", 1), send(near[3], "y", -1), send(near[2], "y", 2)
    x1 = send(pair, "xl", 1)
    m0 = near[0] + q1 + q3 + q2
    both = pair + jnp.concatenate([x1[32:], x1[:32]])

    c3, c1, c2 = send(m0, "y", 1), send(m0, "y", -1), send(m0, "y", 2)
    row = jnp.concatenate([m0, c1, c2, c3])
    rest = send(row, "xl", 1)
    e3, e1, e2 = send(both, "y", 1), send(both, "y", -1), send(both, "y", 2)

    ends = []
    for layout, pieces in (
        ([[(d, 0) for d in range(Y)], [(d, 1) for d in range(Y)]], (row, rest)),
        ([[(d, e) for e in range(XL)] for d in range(Y)], (both, e1, e2, e3)),
    ):
        kept, gone = gradients(softness, layout, pieces, risk)
        came = send(gone, "c", 1)
        width = n_inst + EXT
        *z, acc = call(core_kernel, [(8, width)] * 2 + [(16, width)] * 7 + [(8, EXT)], kept, came)
        z4a, z4b, z0, z1, z2, z3, z5, z6, z7 = z
        shapes = [(16, width)] * 2 + [(8, EXT)]
        up, down = send(z4a, "z", 1), send(z4b, "z", -1)
        up, down, acc = call(first_kernel, shapes, z3, up, z5, down, acc)
        for a, b in ((z2, z6), (z1, z7)):
            up, down = send(up, "z", 1), send(down, "z", -1)
            up, down, acc = call(next_kernel, shapes, a, up, b, down, acc)
        up, down = send(up, "z", 1), send(down, "z", -1)
        keep, go = call(last_kernel, [(8, width)] * 2, z0, up, down, acc)
        ends += [keep, send(go, "xh", 1)]
    last = functools.partial(end_kernel, scenarios)
    gradient, margin = call(last, [(16, n_inst), (16, EXT)], *ends)
    margin = margin[:, 96:100].reshape(2, 8, 4).transpose(2, 0, 1).reshape(64)
    return margin, gradient


def solution(mesh):
    torus = Mesh(mesh.devices.reshape(Y, XL, XH, Z, C), ("y", "xl", "xh", "z", "c"))
    inst, scen = ("y", "xl"), ("xh", "z", "c")
    return jax.shard_map(
        body,
        mesh=torus,
        in_specs=(P(None, inst), P(None, inst), P(inst, scen)),
        out_specs=(P(inst), P(scen, inst)),
        check_vma=False,
    )
```

time: 192 us -> 113 us (0.59)
  blocking collectives: 145 us -> 0 us
  starting transfers between devices: 0 us -> 57.7 us
  matrix products: 34.4 us -> 0 us
  waiting for transfers between devices: 0 us -> 29.8 us
  Pallas kernels: 0 us -> 23.8 us
  other arithmetic: 6.95 us -> 0.21 us
  local copies, waits for them, and re-layouts: 3.73 us -> 0.79 us
    all_to_all x5 -> x0, blocking collectives: 145 us -> none  [the longest x1 54.5 us: summed_rows(): lax.all_to_all(nearer, far, split_axis=0, concat_axis=0, tiled=True)]
    ppermute x0 -> x35, starting transfers between devices: none -> 57.7 us  [send(): return lax.ppermute(x, axis, [(i, (i + shift) % n) for i in range(n)])]
    dot_general x2 -> x0, matrix products: 34.4 us -> none  [the longest x1 18.3 us: body(): jnp.dot(selected_tail, risk, precision=lax.Precision.HIGHEST, preferred_e...]
    ppermute x0 -> x35, waiting for transfers between devices: none -> 29.8 us  [send(): return lax.ppermute(x, axis, [(i, (i + shift) % n) for i in range(n)])]
    pallas_call x0 -> x14, Pallas kernels: none -> 23.8 us  [the longest x2 12.3 us: gradients(): pl.pallas_call(functools.partial(grad_kernel, softness, layout), out_shap...]
    reduce_sum x4 -> x0, other arithmetic: 5.41 us -> none  [the longest x2 2.85 us: sum_at_owner(): return jnp.sum(blocks, axis=0)]
  transfers between devices with their start and end apart: 0 -> 35, of which waited for: 0 -> 18; matrix products, arithmetic and copies ran while one was open for 0% -> 0% of each run, Pallas kernels for 0% -> 12%
where the time goes in v1:
time: 113 us
  starting transfers between devices  57.7 us (51%)
  waiting for transfers between devices  29.8 us (26%)
  Pallas kernels  23.8 us (21%)
    ppermute x35, starting transfers between devices, send(): return lax.ppermute(x, axis, [(i, (i + shift) % n) for i in range(n)])  57.7 us
    ppermute x35, waiting for transfers between devices, send(): return lax.ppermute(x, axis, [(i, (i + shift) % n) for i in range(n)])  29.8 us
    pallas_call x2, Pallas kernels, gradients(): pl.pallas_call(functools.partial(grad_kernel, softness, layout), out_shap...  12.3 us
    pallas_call x1, Pallas kernels, profits(): pl.pallas_call(pnl_kernel, out_shape=[shape(128), shape(128)] + [shape(64...  9.38 us
  transfers between devices with their start and end apart: 35, of which 18 were waited for; matrix products, arithmetic and copies ran while one was open for 0% of the time, Pallas kernels for 12%

profile of v1, /device:TPU:2, one launch (start us, length us, event | category | flops | bytes accessed | tf_op | source)
XLA Modules:
  0.0 113.2 jit_solution(15327795574079827456)
XLA Ops:
  0.6 9.4 %shard_map.50 = (f32[128,1024]{1,0:T(8,128)S(1)}, f32[128,1024]{1,0:T(8,128)S(1)}, f32[64,1024]{1,0:T(8,128)S(1)}, f32[64,1024]{1,0:T(8,128)S(1)}, f32[64,1024]{1,0:T(8,128)S(1)}, /*index=5*/f32[64,1024]{1,0:T(8,128)S(1)}) custom-call(s32[512,2048]{1,0:T(8,128)} %pos.1, s32[8,16]{1,0:T(8,128)} %grid_in.1, f32[2048,1024]{1,0:T(8,128)} %refs_4_.1), custom_call_target="tpu_custom_call" | custom-call | flops 4294967296 | bytes 12582912 | tf_op jit(solution)/shard_map/pallas_call | solution.py:87
  10.0 1.7 %collective-permute-start.18 = (f32[64,1024]{1,0:T(8,128)S(1)}, f32[64,1024]{1,0:T(8,128)S(1)}, u32[]{:S(2)}, u32[]{:S(2)}) collective-permute-start(f32[64,1024]{1,0:T(8,128)S(1)} %get-tuple-element.82), channel_id=1, source_target_pairs={{0,64},{64,128},{128,192},{192,0},{1,65},{65,129},{129,193},{193,1... | collective-permute-start | bytes 786440 | tf_op jit(solution)/shard_map/ppermute | solution.py:22
  11.7 1.7 %collective-permute-start.19 = (f32[64,1024]{1,0:T(8,128)S(1)}, f32[64,1024]{1,0:T(8,128)S(1)}, u32[]{:S(2)}, u32[]{:S(2)}) collective-permute-start(f32[64,1024]{1,0:T(8,128)S(1)} %get-tuple-element.83), channel_id=1, source_target_pairs={{0,192},{64,0},{128,64},{192,128},{1,193},{65,1},{129,65},{193,129... | collective-permute-start | bytes 786440 | tf_op jit(solution)/shard_map/ppermute | solution.py:22
  13.3 2.0 %collective-permute-start.20 = (f32[64,1024]{1,0:T(8,128)S(1)}, f32[64,1024]{1,0:T(8,128)S(1)}, u32[]{:S(2)}, u32[]{:S(2)}) collective-permute-start(f32[64,1024]{1,0:T(8,128)S(1)} %get-tuple-element.84), channel_id=1, source_target_pairs={{0,128},{64,192},{128,0},{192,64},{1,129},{65,193},{129,1},{193,65... | collective-permute-start | bytes 786440 | tf_op jit(solution)/shard_map/ppermute | solution.py:22
  15.3 0.5 collective-permute-start
  15.9 3.6 %collective-permute-done.18 = f32[64,1024]{1,0:T(8,128)S(1)} collective-permute-done((f32[64,1024]{1,0:T(8,128)S(1)}, f32[64,1024]{1,0:T(8,128)S(1)}, u32[]{:S(2)}, u32[]{:S(2)}) %collective-permute-start.18) | collective-permute-done | bytes 262176 | tf_op jit(solution)/shard_map/ppermute | solution.py:22
  19.4 5.0 %collective-permute-done.19 = f32[64,1024]{1,0:T(8,128)S(1)} collective-permute-done((f32[64,1024]{1,0:T(8,128)S(1)}, f32[64,1024]{1,0:T(8,128)S(1)}, u32[]{:S(2)}, u32[]{:S(2)}) %collective-permute-start.19) | collective-permute-done | bytes 262176 | tf_op jit(solution)/shard_map/ppermute | solution.py:22
  24.4 1.8 %collective-permute-done.20 = f32[64,1024]{1,0:T(8,128)S(1)} collective-permute-done((f32[64,1024]{1,0:T(8,128)S(1)}, f32[64,1024]{1,0:T(8,128)S(1)}, u32[]{:S(2)}, u32[]{:S(2)}) %collective-permute-start.20) | collective-permute-done | bytes 262176 | tf_op jit(solution)/shard_map/ppermute | solution.py:22
  26.3 0.6 collective-permute-start.21
  26.9 1.5 %collective-permute-done = f32[128,1024]{1,0:T(8,128)S(1)} collective-permute-done((f32[128,1024]{1,0:T(8,128)S(1)}, f32[128,1024]{1,0:T(8,128)S(1)}, u32[]{:S(2)}, u32[]{:S(2)}) %collective-permute-start) | collective-permute-done | bytes 524320 | tf_op jit(solution)/shard_map/ppermute | solution.py:22
  28.4 0.6 collective-permute-start.1
  29.0 2.3 %collective-permute-start.3 = (f32[32,1024]{1,0:T(8,128)S(1)}, f32[32,1024]{1,0:T(8,128)S(1)}, u32[]{:S(2)}, u32[]{:S(2)}) collective-permute-start(f32[32,1024]{1,0:T(8,128)S(1)} %get-tuple-element.111), channel_id=1, source_target_pairs={{0,128},{64,192},{128,0},{192,64},{1,129},{65,193},{129,1},{193,65... | collective-permute-start | bytes 393224 | tf_op jit(solution)/shard_map/ppermute | solution.py:22
  31.3 2.5 %collective-permute-start.2 = (f32[32,1024]{1,0:T(8,128)S(1)}, f32[32,1024]{1,0:T(8,128)S(1)}, u32[]{:S(2)}, u32[]{:S(2)}) collective-permute-start(f32[32,1024]{1,0:T(8,128)S(1)} %get-tuple-element.112), channel_id=1, source_target_pairs={{0,192},{64,0},{128,64},{192,128},{1,193},{65,1},{129,65},{193,129... | collective-permute-start | bytes 393224 | tf_op jit(solution)/shard_map/ppermute | solution.py:22
  33.9 2.2 %collective-permute-done.1 = f32[32,1024]{1,0:T(8,128)S(1)} collective-permute-done((f32[32,1024]{1,0:T(8,128)S(1)}, f32[32,1024]{1,0:T(8,128)S(1)}, u32[]{:S(2)}, u32[]{:S(2)}) %collective-permute-start.1) | collective-permute-done | bytes 131104 | tf_op jit(solution)/shard_map/ppermute | solution.py:22
  36.1 0.9 collective-permute-done.2
  37.0 2.1 %collective-permute-start.6 = (f32[32,1024]{1,0:T(8,128)S(1)}, f32[32,1024]{1,0:T(8,128)S(1)}, u32[]{:S(2)}, u32[]{:S(2)}) collective-permute-start(f32[32,1024]{1,0:T(8,128)S(1)} %fusion.2), channel_id=1, source_target_pairs={{0,64},{64,128},{128,192},{192,0},{1,65},{65,129},{129,193},{193,1... | collective-permute-start | bytes 393224 | tf_op jit(solution)/shard_map/ppermute | solution.py:22
  39.1 2.5 %collective-permute-start.5 = (f32[32,1024]{1,0:T(8,128)S(1)}, f32[32,1024]{1,0:T(8,128)S(1)}, u32[]{:S(2)}, u32[]{:S(2)}) collective-permute-start(f32[32,1024]{1,0:T(8,128)S(1)} %fusion.2), channel_id=1, source_target_pairs={{0,128},{64,192},{128,0},{192,64},{1,129},{65,193},{129,1},{193,65... | collective-permute-start | bytes 393224 | tf_op jit(solution)/shard_map/ppermute | solution.py:22
  41.6 0.8 collective-permute-start.4
  42.5 1.3 %collective-permute-start.24 = (f32[64,1024]{1,0:T(8,128)S(1)}, f32[64,1024]{1,0:T(8,128)S(1)}, u32[]{:S(2)}, u32[]{:S(2)}) collective-permute-start(f32[64,1024]{1,0:T(8,128)S(1)} %maximum_add_fusion.refs_0_), channel_id=1, source_target_pairs={{0,64},{64,128},{128,192},{192,0},{1,65},{65,129},{129,193},{193,1... | collective-permute-start | bytes 786440 | tf_op jit(solution)/shard_map/ppermute | solution.py:22
  43.7 1.0 collective-permute-start.23
  44.7 1.8 %collective-permute-start.22 = (f32[64,1024]{1,0:T(8,128)S(1)}, f32[64,1024]{1,0:T(8,128)S(1)}, u32[]{:S(2)}, u32[]{:S(2)}) collective-permute-start(f32[64,1024]{1,0:T(8,128)S(1)} %maximum_add_fusion.refs_0_), channel_id=1, source_target_pairs={{0,192},{64,0},{128,64},{192,128},{1,193},{65,1},{129,65},{193,129... | collective-permute-start | bytes 786440 | tf_op jit(solution)/shard_map/ppermute | solution.py:22
  46.5 2.3 %collective-permute-done.5 = f32[32,1024]{1,0:T(8,128)S(1)} collective-permute-done((f32[32,1024]{1,0:T(8,128)S(1)}, f32[32,1024]{1,0:T(8,128)S(1)}, u32[]{:S(2)}, u32[]{:S(2)}) %collective-permute-start.5) | collective-permute-done | bytes 131104 | tf_op jit(solution)/shard_map/ppermute | solution.py:22
  48.9 0.9 collective-permute-start.7
  49.8 2.6 %collective-permute-done.24.refs_3_ = f32[64,1024]{1,0:T(8,128)S(1)} collective-permute-done((f32[64,1024]{1,0:T(8,128)S(1)}, f32[64,1024]{1,0:T(8,128)S(1)}, u32[]{:S(2)}, u32[]{:S(2)}) %collective-permute-start.24) | collective-permute-done | bytes 262176 | tf_op jit(solution)/shard_map/ppermute | solution.py:22
  52.4 2.8 %collective-permute-done.23.refs_2_ = f32[64,1024]{1,0:T(8,128)S(1)} collective-permute-done((f32[64,1024]{1,0:T(8,128)S(1)}, f32[64,1024]{1,0:T(8,128)S(1)}, u32[]{:S(2)}, u32[]{:S(2)}) %collective-permute-start.23) | collective-permute-done | bytes 262176 | tf_op jit(solution)/shard_map/ppermute | solution.py:22
  55.2 0.6 collective-permute-done.22.refs_1_
  55.8 6.1 %shard_map.57 = (f32[128,2176]{1,0:T(8,128)S(1)}, f32[128,2176]{1,0:T(8,128)S(1)}) custom-call(f32[64,1024]{1,0:T(8,128)S(1)} %maximum_add_fusion.refs_0_, f32[64,1024]{1,0:T(8,128)S(1)} %collective-permute-done.22.refs_1_, f32[64,1024]{1,0:T(8,128)S(1)} %collective-permute-done.23.refs_2_, f32[64,1024]{1,0:T(8,128)S(1)} %collective-permute-done.24.refs_3_, ...), custom_call_target="tpu_custom_call" | custom-call | flops 3221225472 | bytes 8388608 | tf_op jit(solution)/shard_map/pallas_call | solution.py:173
  62.0 0.1 collective-permute-start.25
  62.1 6.2 %shard_map.51 = (f32[128,2176]{1,0:T(8,128)S(1)}, f32[128,2176]{1,0:T(8,128)S(1)}) custom-call(f32[128,1024]{1,0:T(8,128)S(1)} %pad_maximum_fusion.refs_0_, f32[128,1024]{1,0:T(8,128)S(1)} %collective-permute-done.7.refs_1_, f32[2048,1024]{1,0:T(8,128)S(1)} %copy-done), custom_call_target="tpu_custom_call" | custom-call | flops 3221225472 | bytes 8388608 | tf_op jit(solution)/shard_map/pallas_call | solution.py:173
  68.3 0.5 collective-permute-start.8
  68.8 0.2 shard_map.58
  69.1 2.2 %collective-permute-start.26 = (f32[8,2176]{1,0:T(8,128)S(1)}, f32[8,2176]{1,0:T(8,128)S(1)}, u32[]{:S(2)}, u32[]{:S(2)}) collective-permute-start(f32[8,2176]{1,0:T(8,128)S(1)} %get-tuple-element.91), channel_id=1, source_target_pairs={{0,2},{2,4},{4,6},{6,8},{8,10},{10,12},{12,14},{14,0},{1,3},{3,5},... | collective-permute-start | bytes 208904 | tf_op jit(solution)/shard_map/ppermute | solution.py:22
  71.3 4.0 %collective-permute-start.27 = (f32[8,2176]{1,0:T(8,128)S(1)}, f32[8,2176]{1,0:T(8,128)S(1)}, u32[]{:S(2)}, u32[]{:S(2)}) collective-permute-start(f32[8,2176]{1,0:T(8,128)S(1)} %get-tuple-element.93), channel_id=1, source_target_pairs={{0,14},{2,0},{4,2},{6,4},{8,6},{10,8},{12,10},{14,12},{1,15},{3,1}... | collective-permute-start | bytes 208904 | tf_op jit(solution)/shard_map/ppermute | solution.py:22
  75.3 0.2 shard_map.52
  75.6 3.2 %collective-permute-start.10 = (f32[8,2176]{1,0:T(8,128)S(1)}, f32[8,2176]{1,0:T(8,128)S(1)}, u32[]{:S(2)}, u32[]{:S(2)}) collective-permute-start(f32[8,2176]{1,0:T(8,128)S(1)} %get-tuple-element.66), channel_id=1, source_target_pairs={{0,14},{2,0},{4,2},{6,4},{8,6},{10,8},{12,10},{14,12},{1,15},{3,1}... | collective-permute-start | bytes 208904 | tf_op jit(solution)/shard_map/ppermute | solution.py:22
  78.9 0.1 shard_map.59
  79.1 3.2 %collective-permute-start.29 = (f32[16,2176]{1,0:T(8,128)S(1)}, f32[16,2176]{1,0:T(8,128)S(1)}, u32[]{:S(2)}, u32[]{:S(2)}) collective-permute-start(f32[16,2176]{1,0:T(8,128)S(1)} %get-tuple-element.97), channel_id=1, source_target_pairs={{0,14},{2,0},{4,2},{6,4},{8,6},{10,8},{12,10},{14,12},{1,15},{3,1}... | collective-permute-start | bytes 417800 | tf_op jit(solution)/shard_map/ppermute | solution.py:22
  82.3 0.1 shard_map.53
  82.5 3.2 %collective-permute-start.12 = (f32[16,2176]{1,0:T(8,128)S(1)}, f32[16,2176]{1,0:T(8,128)S(1)}, u32[]{:S(2)}, u32[]{:S(2)}) collective-permute-start(f32[16,2176]{1,0:T(8,128)S(1)} %get-tuple-element.70), channel_id=1, source_target_pairs={{0,14},{2,0},{4,2},{6,4},{8,6},{10,8},{12,10},{14,12},{1,15},{3,1}... | collective-permute-start | bytes 417800 | tf_op jit(solution)/shard_map/ppermute | solution.py:22
  85.7 0.1 shard_map.60
  85.8 2.2 %collective-permute-start.30 = (f32[16,2176]{1,0:T(8,128)S(1)}, f32[16,2176]{1,0:T(8,128)S(1)}, u32[]{:S(2)}, u32[]{:S(2)}) collective-permute-start(f32[16,2176]{1,0:T(8,128)S(1)} %get-tuple-element.99), channel_id=1, source_target_pairs={{0,2},{2,4},{4,6},{6,8},{8,10},{10,12},{12,14},{14,0},{1,3},{3,5},... | collective-permute-start | bytes 417800 | tf_op jit(solution)/shard_map/ppermute | solution.py:22
  88.0 1.5 %collective-permute-start.31 = (f32[16,2176]{1,0:T(8,128)S(1)}, f32[16,2176]{1,0:T(8,128)S(1)}, u32[]{:S(2)}, u32[]{:S(2)}) collective-permute-start(f32[16,2176]{1,0:T(8,128)S(1)} %get-tuple-element.101), channel_id=1, source_target_pairs={{0,14},{2,0},{4,2},{6,4},{8,6},{10,8},{12,10},{14,12},{1,15},{3,1}... | collective-permute-start | bytes 417800 | tf_op jit(solution)/shard_map/ppermute | solution.py:22
  89.5 0.2 collective-permute-done.11.up
  89.7 0.1 shard_map.54
  89.8 1.9 %collective-permute-start.13 = (f32[16,2176]{1,0:T(8,128)S(1)}, f32[16,2176]{1,0:T(8,128)S(1)}, u32[]{:S(2)}, u32[]{:S(2)}) collective-permute-start(f32[16,2176]{1,0:T(8,128)S(1)} %get-tuple-element.72), channel_id=1, source_target_pairs={{0,2},{2,4},{4,6},{6,8},{8,10},{10,12},{12,14},{14,0},{1,3},{3,5},... | collective-permute-start | bytes 417800 | tf_op jit(solution)/shard_map/ppermute | solution.py:22
  91.7 2.0 %collective-permute-start.14 = (f32[16,2176]{1,0:T(8,128)S(1)}, f32[16,2176]{1,0:T(8,128)S(1)}, u32[]{:S(2)}, u32[]{:S(2)}) collective-permute-start(f32[16,2176]{1,0:T(8,128)S(1)} %get-tuple-element.74), channel_id=1, source_target_pairs={{0,14},{2,0},{4,2},{6,4},{8,6},{10,8},{12,10},{14,12},{1,15},{3,1}... | collective-permute-start | bytes 417800 | tf_op jit(solution)/shard_map/ppermute | solution.py:22
  93.8 0.6 collective-permute-done.31.down
  94.3 0.1 shard_map.61
  94.4 2.6 %collective-permute-start.32 = (f32[16,2176]{1,0:T(8,128)S(1)}, f32[16,2176]{1,0:T(8,128)S(1)}, u32[]{:S(2)}, u32[]{:S(2)}) collective-permute-start(f32[16,2176]{1,0:T(8,128)S(1)} %get-tuple-element.103), channel_id=1, source_target_pairs={{0,2},{2,4},{4,6},{6,8},{8,10},{10,12},{12,14},{14,0},{1,3},{3,5},... | collective-permute-start | bytes 417800 | tf_op jit(solution)/shard_map/ppermute | solution.py:22
  97.0 0.7 collective-permute-start.33
  97.7 0.2 collective-permute-done.14.down
  97.9 0.1 shard_map.55
  98.1 2.4 %collective-permute-start.15 = (f32[16,2176]{1,0:T(8,128)S(1)}, f32[16,2176]{1,0:T(8,128)S(1)}, u32[]{:S(2)}, u32[]{:S(2)}) collective-permute-start(f32[16,2176]{1,0:T(8,128)S(1)} %get-tuple-element.76), channel_id=1, source_target_pairs={{0,2},{2,4},{4,6},{6,8},{8,10},{10,12},{12,14},{14,0},{1,3},{3,5},... | collective-permute-start | bytes 417800 | tf_op jit(solution)/shard_map/ppermute | solution.py:22
  100.5 0.9 collective-permute-start.16
  101.4 0.7 collective-permute-done.33.down
  102.1 0.1 shard_map.62
  102.2 2.2 %collective-permute-start.34 = (f32[8,2176]{1,0:T(8,128)S(1)}, f32[8,2176]{1,0:T(8,128)S(1)}, u32[]{:S(2)}, u32[]{:S(2)}) collective-permute-start(f32[8,2176]{1,0:T(8,128)S(1)} %get-tuple-element.107), channel_id=1, source_target_pairs={{0,16},{16,0},{1,17},{17,1},{2,18},{18,2},{3,19},{19,3},{4,20},{20... | collective-permute-start | bytes 208904 | tf_op jit(solution)/shard_map/ppermute | solution.py:22
  104.4 1.1 %collective-permute-done.16.down = f32[16,2176]{1,0:T(8,128)S(1)} collective-permute-done((f32[16,2176]{1,0:T(8,128)S(1)}, f32[16,2176]{1,0:T(8,128)S(1)}, u32[]{:S(2)}, u32[]{:S(2)}) %collective-permute-start.16) | collective-permute-done | bytes 139296 | tf_op jit(solution)/shard_map/ppermute | solution.py:22
  105.5 0.1 shard_map.56
  105.7 2.2 %collective-permute-start.17 = (f32[8,2176]{1,0:T(8,128)S(1)}, f32[8,2176]{1,0:T(8,128)S(1)}, u32[]{:S(2)}, u32[]{:S(2)}) collective-permute-start(f32[8,2176]{1,0:T(8,128)S(1)} %get-tuple-element.80), channel_id=1, source_target_pairs={{0,16},{16,0},{1,17},{17,1},{2,18},{18,2},{3,19},{19,3},{4,20},{20... | collective-permute-start | bytes 208904 | tf_op jit(solution)/shard_map/ppermute | solution.py:22
  107.8 0.2 collective-permute-done.34.came1
  108.1 3.5 %collective-permute-done.17.came0 = f32[8,2176]{1,0:T(8,128)S(1)} collective-permute-done((f32[8,2176]{1,0:T(8,128)S(1)}, f32[8,2176]{1,0:T(8,128)S(1)}, u32[]{:S(2)}, u32[]{:S(2)}) %collective-permute-start.17) | collective-permute-done | bytes 69664 | tf_op jit(solution)/shard_map/ppermute | solution.py:22
  111.6 0.8 shard_map.63
  112.6 0.6 reshape.11
  (31 shorter events, 0.8 us)
Async XLA Ops:
  0.6 55.2 %copy-start = (f32[2048,1024]{1,0:T(8,128)S(1)}, f32[2048,1024]{1,0:T(8,128)}, u32[]{:S(2)}) copy-start(f32[2048,1024]{1,0:T(8,128)} %refs_4_.1) | copy-start | bytes 25165828
  10.0 9.4 %collective-permute-start.18 = (f32[64,1024]{1,0:T(8,128)S(1)}, f32[64,1024]{1,0:T(8,128)S(1)}, u32[]{:S(2)}, u32[]{:S(2)}) collective-permute-start(f32[64,1024]{1,0:T(8,128)S(1)} %get-tuple-element.82), channel_id=1, source_target_pairs={{0,64},{64,128},{128,192},{192,0},{1,65},{65,129},{129,193},{193,1... | collective-permute-start | bytes 786440 | tf_op jit(solution)/shard_map/ppermute | solution.py:22
  11.7 12.7 %collective-permute-start.19 = (f32[64,1024]{1,0:T(8,128)S(1)}, f32[64,1024]{1,0:T(8,128)S(1)}, u32[]{:S(2)}, u32[]{:S(2)}) collective-permute-start(f32[64,1024]{1,0:T(8,128)S(1)} %get-tuple-element.83), channel_id=1, source_target_pairs={{0,192},{64,0},{128,64},{192,128},{1,193},{65,1},{129,65},{193,129... | collective-permute-start | bytes 786440 | tf_op jit(solution)/shard_map/ppermute | solution.py:22
  13.3 12.9 %collective-permute-start.20 = (f32[64,1024]{1,0:T(8,128)S(1)}, f32[64,1024]{1,0:T(8,128)S(1)}, u32[]{:S(2)}, u32[]{:S(2)}) collective-permute-start(f32[64,1024]{1,0:T(8,128)S(1)} %get-tuple-element.84), channel_id=1, source_target_pairs={{0,128},{64,192},{128,0},{192,64},{1,129},{65,193},{129,1},{193,65... | collective-permute-start | bytes 786440 | tf_op jit(solution)/shard_map/ppermute | solution.py:22
  15.3 13.0 %collective-permute-start = (f32[128,1024]{1,0:T(8,128)S(1)}, f32[128,1024]{1,0:T(8,128)S(1)}, u32[]{:S(2)}, u32[]{:S(2)}) collective-permute-start(f32[128,1024]{1,0:T(8,128)S(1)} %get-tuple-element.57), channel_id=1, source_target_pairs={{0,32},{32,0},{1,33},{33,1},{2,34},{34,2},{3,35},{35,3},{4,36},{36... | collective-permute-start | bytes 1572872 | tf_op jit(solution)/shard_map/ppermute | solution.py:22
  26.3 7.6 %collective-permute-start.21 = (f32[64,1024]{1,0:T(8,128)S(1)}, f32[64,1024]{1,0:T(8,128)S(1)}, u32[]{:S(2)}, u32[]{:S(2)}) collective-permute-start(f32[64,1024]{1,0:T(8,128)S(1)} %add_add_fusion), channel_id=1, source_target_pairs={{0,32},{32,0},{1,33},{33,1},{2,34},{34,2},{3,35},{35,3},{4,36},{36... | collective-permute-start | bytes 786440 | tf_op jit(solution)/shard_map/ppermute | solution.py:22
  28.4 7.7 %collective-permute-start.1 = (f32[32,1024]{1,0:T(8,128)S(1)}, f32[32,1024]{1,0:T(8,128)S(1)}, u32[]{:S(2)}, u32[]{:S(2)}) collective-permute-start(f32[32,1024]{1,0:T(8,128)S(1)} %get-tuple-element.110), channel_id=1, source_target_pairs={{0,64},{64,128},{128,192},{192,0},{1,65},{65,129},{129,193},{193,1... | collective-permute-start | bytes 393224 | tf_op jit(solution)/shard_map/ppermute | solution.py:22
  29.0 7.1 %collective-permute-start.3 = (f32[32,1024]{1,0:T(8,128)S(1)}, f32[32,1024]{1,0:T(8,128)S(1)}, u32[]{:S(2)}, u32[]{:S(2)}) collective-permute-start(f32[32,1024]{1,0:T(8,128)S(1)} %get-tuple-element.111), channel_id=1, source_target_pairs={{0,128},{64,192},{128,0},{192,64},{1,129},{65,193},{129,1},{193,65... | collective-permute-start | bytes 393224 | tf_op jit(solution)/shard_map/ppermute | solution.py:22
  31.3 5.6 %collective-permute-start.2 = (f32[32,1024]{1,0:T(8,128)S(1)}, f32[32,1024]{1,0:T(8,128)S(1)}, u32[]{:S(2)}, u32[]{:S(2)}) collective-permute-start(f32[32,1024]{1,0:T(8,128)S(1)} %get-tuple-element.112), channel_id=1, source_target_pairs={{0,192},{64,0},{128,64},{192,128},{1,193},{65,1},{129,65},{193,129... | collective-permute-start | bytes 393224 | tf_op jit(solution)/shard_map/ppermute | solution.py:22
  37.0 7.8 %collective-permute-start.6 = (f32[32,1024]{1,0:T(8,128)S(1)}, f32[32,1024]{1,0:T(8,128)S(1)}, u32[]{:S(2)}, u32[]{:S(2)}) collective-permute-start(f32[32,1024]{1,0:T(8,128)S(1)} %fusion.2), channel_id=1, source_target_pairs={{0,64},{64,128},{128,192},{192,0},{1,65},{65,129},{129,193},{193,1... | collective-permute-start | bytes 393224 | tf_op jit(solution)/shard_map/ppermute | solution.py:22
  39.1 9.8 %collective-permute-start.5 = (f32[32,1024]{1,0:T(8,128)S(1)}, f32[32,1024]{1,0:T(8,128)S(1)}, u32[]{:S(2)}, u32[]{:S(2)}) collective-permute-start(f32[32,1024]{1,0:T(8,128)S(1)} %fusion.2), channel_id=1, source_target_pairs={{0,128},{64,192},{128,0},{192,64},{1,129},{65,193},{129,1},{193,65... | collective-permute-start | bytes 393224 | tf_op jit(solution)/shard_map/ppermute | solution.py:22
  41.6 7.3 %collective-permute-start.4 = (f32[32,1024]{1,0:T(8,128)S(1)}, f32[32,1024]{1,0:T(8,128)S(1)}, u32[]{:S(2)}, u32[]{:S(2)}) collective-permute-start(f32[32,1024]{1,0:T(8,128)S(1)} %fusion.2), channel_id=1, source_target_pairs={{0,192},{64,0},{128,64},{192,128},{1,193},{65,1},{129,65},{193,129... | collective-permute-start | bytes 393224 | tf_op jit(solution)/shard_map/ppermute | solution.py:22
  42.5 9.9 %collective-permute-start.24 = (f32[64,1024]{1,0:T(8,128)S(1)}, f32[64,1024]{1,0:T(8,128)S(1)}, u32[]{:S(2)}, u32[]{:S(2)}) collective-permute-start(f32[64,1024]{1,0:T(8,128)S(1)} %maximum_add_fusion.refs_0_), channel_id=1, source_target_pairs={{0,64},{64,128},{128,192},{192,0},{1,65},{65,129},{129,193},{193,1... | collective-permute-start | bytes 786440 | tf_op jit(solution)/shard_map/ppermute | solution.py:22
  43.7 11.5 %collective-permute-start.23 = (f32[64,1024]{1,0:T(8,128)S(1)}, f32[64,1024]{1,0:T(8,128)S(1)}, u32[]{:S(2)}, u32[]{:S(2)}) collective-permute-start(f32[64,1024]{1,0:T(8,128)S(1)} %maximum_add_fusion.refs_0_), channel_id=1, source_target_pairs={{0,128},{64,192},{128,0},{192,64},{1,129},{65,193},{129,1},{193,65... | collective-permute-start | bytes 786440 | tf_op jit(solution)/shard_map/ppermute | solution.py:22
  44.7 11.1 %collective-permute-start.22 = (f32[64,1024]{1,0:T(8,128)S(1)}, f32[64,1024]{1,0:T(8,128)S(1)}, u32[]{:S(2)}, u32[]{:S(2)}) collective-permute-start(f32[64,1024]{1,0:T(8,128)S(1)} %maximum_add_fusion.refs_0_), channel_id=1, source_target_pairs={{0,192},{64,0},{128,64},{192,128},{1,193},{65,1},{129,65},{193,129... | collective-permute-start | bytes 786440 | tf_op jit(solution)/shard_map/ppermute | solution.py:22
  48.9 13.2 %collective-permute-start.7 = (f32[128,1024]{1,0:T(8,128)S(1)}, f32[128,1024]{1,0:T(8,128)S(1)}, u32[]{:S(2)}, u32[]{:S(2)}) collective-permute-start(f32[128,1024]{1,0:T(8,128)S(1)} %pad_maximum_fusion.refs_0_), channel_id=1, source_target_pairs={{0,32},{32,0},{1,33},{33,1},{2,34},{34,2},{3,35},{35,3},{4,36},{36... | collective-permute-start | bytes 1572872 | tf_op jit(solution)/shard_map/ppermute | solution.py:22
  62.0 6.8 %collective-permute-start.25 = (f32[128,2176]{1,0:T(8,128)S(1)}, f32[128,2176]{1,0:T(8,128)S(1)}, u32[]{:S(2)}, u32[]{:S(2)}) collective-permute-start(f32[128,2176]{1,0:T(8,128)S(1)} %get-tuple-element.86), channel_id=1, source_target_pairs={{0,1},{1,0},{2,3},{3,2},{4,5},{5,4},{6,7},{7,6},{8,9},{9,8},{10,11... | collective-permute-start | bytes 3342344 | tf_op jit(solution)/shard_map/ppermute | solution.py:22
  68.3 7.0 %collective-permute-start.8 = (f32[128,2176]{1,0:T(8,128)S(1)}, f32[128,2176]{1,0:T(8,128)S(1)}, u32[]{:S(2)}, u32[]{:S(2)}) collective-permute-start(f32[128,2176]{1,0:T(8,128)S(1)} %get-tuple-element.59), channel_id=1, source_target_pairs={{0,1},{1,0},{2,3},{3,2},{4,5},{5,4},{6,7},{7,6},{8,9},{9,8},{10,11... | collective-permute-start | bytes 3342344 | tf_op jit(solution)/shard_map/ppermute | solution.py:22
  69.1 9.8 %collective-permute-start.26 = (f32[8,2176]{1,0:T(8,128)S(1)}, f32[8,2176]{1,0:T(8,128)S(1)}, u32[]{:S(2)}, u32[]{:S(2)}) collective-permute-start(f32[8,2176]{1,0:T(8,128)S(1)} %get-tuple-element.91), channel_id=1, source_target_pairs={{0,2},{2,4},{4,6},{6,8},{8,10},{10,12},{12,14},{14,0},{1,3},{3,5},... | collective-permute-start | bytes 208904 | tf_op jit(solution)/shard_map/ppermute | solution.py:22
  71.3 7.6 %collective-permute-start.27 = (f32[8,2176]{1,0:T(8,128)S(1)}, f32[8,2176]{1,0:T(8,128)S(1)}, u32[]{:S(2)}, u32[]{:S(2)}) collective-permute-start(f32[8,2176]{1,0:T(8,128)S(1)} %get-tuple-element.93), channel_id=1, source_target_pairs={{0,14},{2,0},{4,2},{6,4},{8,6},{10,8},{12,10},{14,12},{1,15},{3,1}... | collective-permute-start | bytes 208904 | tf_op jit(solution)/shard_map/ppermute | solution.py:22
  75.5 6.7 %collective-permute-start.9 = (f32[8,2176]{1,0:T(8,128)S(1)}, f32[8,2176]{1,0:T(8,128)S(1)}, u32[]{:S(2)}, u32[]{:S(2)}) collective-permute-start(f32[8,2176]{1,0:T(8,128)S(1)} %get-tuple-element.64), channel_id=1, source_target_pairs={{0,2},{2,4},{4,6},{6,8},{8,10},{10,12},{12,14},{14,0},{1,3},{3,5},... | collective-permute-start | bytes 208904 | tf_op jit(solution)/shard_map/ppermute | solution.py:22
  75.6 6.7 %collective-permute-start.10 = (f32[8,2176]{1,0:T(8,128)S(1)}, f32[8,2176]{1,0:T(8,128)S(1)}, u32[]{:S(2)}, u32[]{:S(2)}) collective-permute-start(f32[8,2176]{1,0:T(8,128)S(1)} %get-tuple-element.66), channel_id=1, source_target_pairs={{0,14},{2,0},{4,2},{6,4},{8,6},{10,8},{12,10},{14,12},{1,15},{3,1}... | collective-permute-start | bytes 208904 | tf_op jit(solution)/shard_map/ppermute | solution.py:22
  79.0 6.7 %collective-permute-start.28 = (f32[16,2176]{1,0:T(8,128)S(1)}, f32[16,2176]{1,0:T(8,128)S(1)}, u32[]{:S(2)}, u32[]{:S(2)}) collective-permute-start(f32[16,2176]{1,0:T(8,128)S(1)} %get-tuple-element.95), channel_id=1, source_target_pairs={{0,2},{2,4},{4,6},{6,8},{8,10},{10,12},{12,14},{14,0},{1,3},{3,5},... | collective-permute-start | bytes 417800 | tf_op jit(solution)/shard_map/ppermute | solution.py:22
  79.1 6.7 %collective-permute-start.29 = (f32[16,2176]{1,0:T(8,128)S(1)}, f32[16,2176]{1,0:T(8,128)S(1)}, u32[]{:S(2)}, u32[]{:S(2)}) collective-permute-start(f32[16,2176]{1,0:T(8,128)S(1)} %get-tuple-element.97), channel_id=1, source_target_pairs={{0,14},{2,0},{4,2},{6,4},{8,6},{10,8},{12,10},{14,12},{1,15},{3,1}... | collective-permute-start | bytes 417800 | tf_op jit(solution)/shard_map/ppermute | solution.py:22
  82.4 7.3 %collective-permute-start.11 = (f32[16,2176]{1,0:T(8,128)S(1)}, f32[16,2176]{1,0:T(8,128)S(1)}, u32[]{:S(2)}, u32[]{:S(2)}) collective-permute-start(f32[16,2176]{1,0:T(8,128)S(1)} %get-tuple-element.68), channel_id=1, source_target_pairs={{0,2},{2,4},{4,6},{6,8},{8,10},{10,12},{12,14},{14,0},{1,3},{3,5},... | collective-permute-start | bytes 417800 | tf_op jit(solution)/shard_map/ppermute | solution.py:22
  82.5 7.2 %collective-permute-start.12 = (f32[16,2176]{1,0:T(8,128)S(1)}, f32[16,2176]{1,0:T(8,128)S(1)}, u32[]{:S(2)}, u32[]{:S(2)}) collective-permute-start(f32[16,2176]{1,0:T(8,128)S(1)} %get-tuple-element.70), channel_id=1, source_target_pairs={{0,14},{2,0},{4,2},{6,4},{8,6},{10,8},{12,10},{14,12},{1,15},{3,1}... | collective-permute-start | bytes 417800 | tf_op jit(solution)/shard_map/ppermute | solution.py:22
  85.8 7.9 %collective-permute-start.30 = (f32[16,2176]{1,0:T(8,128)S(1)}, f32[16,2176]{1,0:T(8,128)S(1)}, u32[]{:S(2)}, u32[]{:S(2)}) collective-permute-start(f32[16,2176]{1,0:T(8,128)S(1)} %get-tuple-element.99), channel_id=1, source_target_pairs={{0,2},{2,4},{4,6},{6,8},{8,10},{10,12},{12,14},{14,0},{1,3},{3,5},... | collective-permute-start | bytes 417800 | tf_op jit(solution)/shard_map/ppermute | solution.py:22
  88.0 6.3 %collective-permute-start.31 = (f32[16,2176]{1,0:T(8,128)S(1)}, f32[16,2176]{1,0:T(8,128)S(1)}, u32[]{:S(2)}, u32[]{:S(2)}) collective-permute-start(f32[16,2176]{1,0:T(8,128)S(1)} %get-tuple-element.101), channel_id=1, source_target_pairs={{0,14},{2,0},{4,2},{6,4},{8,6},{10,8},{12,10},{14,12},{1,15},{3,1}... | collective-permute-start | bytes 417800 | tf_op jit(solution)/shard_map/ppermute | solution.py:22
  89.8 8.0 %collective-permute-start.13 = (f32[16,2176]{1,0:T(8,128)S(1)}, f32[16,2176]{1,0:T(8,128)S(1)}, u32[]{:S(2)}, u32[]{:S(2)}) collective-permute-start(f32[16,2176]{1,0:T(8,128)S(1)} %get-tuple-element.72), channel_id=1, source_target_pairs={{0,2},{2,4},{4,6},{6,8},{8,10},{10,12},{12,14},{14,0},{1,3},{3,5},... | collective-permute-start | bytes 417800 | tf_op jit(solution)/shard_map/ppermute | solution.py:22
  91.7 6.2 %collective-permute-start.14 = (f32[16,2176]{1,0:T(8,128)S(1)}, f32[16,2176]{1,0:T(8,128)S(1)}, u32[]{:S(2)}, u32[]{:S(2)}) collective-permute-start(f32[16,2176]{1,0:T(8,128)S(1)} %get-tuple-element.74), channel_id=1, source_target_pairs={{0,14},{2,0},{4,2},{6,4},{8,6},{10,8},{12,10},{14,12},{1,15},{3,1}... | collective-permute-start | bytes 417800 | tf_op jit(solution)/shard_map/ppermute | solution.py:22
  94.4 6.9 %collective-permute-start.32 = (f32[16,2176]{1,0:T(8,128)S(1)}, f32[16,2176]{1,0:T(8,128)S(1)}, u32[]{:S(2)}, u32[]{:S(2)}) collective-permute-start(f32[16,2176]{1,0:T(8,128)S(1)} %get-tuple-element.103), channel_id=1, source_target_pairs={{0,2},{2,4},{4,6},{6,8},{8,10},{10,12},{12,14},{14,0},{1,3},{3,5},... | collective-permute-start | bytes 417800 | tf_op jit(solution)/shard_map/ppermute | solution.py:22
  97.0 5.1 %collective-permute-start.33 = (f32[16,2176]{1,0:T(8,128)S(1)}, f32[16,2176]{1,0:T(8,128)S(1)}, u32[]{:S(2)}, u32[]{:S(2)}) collective-permute-start(f32[16,2176]{1,0:T(8,128)S(1)} %get-tuple-element.104), channel_id=1, source_target_pairs={{0,14},{2,0},{4,2},{6,4},{8,6},{10,8},{12,10},{14,12},{1,15},{3,1}... | collective-permute-start | bytes 417800 | tf_op jit(solution)/shard_map/ppermute | solution.py:22
  98.1 6.3 %collective-permute-start.15 = (f32[16,2176]{1,0:T(8,128)S(1)}, f32[16,2176]{1,0:T(8,128)S(1)}, u32[]{:S(2)}, u32[]{:S(2)}) collective-permute-start(f32[16,2176]{1,0:T(8,128)S(1)} %get-tuple-element.76), channel_id=1, source_target_pairs={{0,2},{2,4},{4,6},{6,8},{8,10},{10,12},{12,14},{14,0},{1,3},{3,5},... | collective-permute-start | bytes 417800 | tf_op jit(solution)/shard_map/ppermute | solution.py:22
  100.5 5.1 %collective-permute-start.16 = (f32[16,2176]{1,0:T(8,128)S(1)}, f32[16,2176]{1,0:T(8,128)S(1)}, u32[]{:S(2)}, u32[]{:S(2)}) collective-permute-start(f32[16,2176]{1,0:T(8,128)S(1)} %get-tuple-element.77), channel_id=1, source_target_pairs={{0,14},{2,0},{4,2},{6,4},{8,6},{10,8},{12,10},{14,12},{1,15},{3,1}... | collective-permute-start | bytes 417800 | tf_op jit(solution)/shard_map/ppermute | solution.py:22
  102.2 5.9 %collective-permute-start.34 = (f32[8,2176]{1,0:T(8,128)S(1)}, f32[8,2176]{1,0:T(8,128)S(1)}, u32[]{:S(2)}, u32[]{:S(2)}) collective-permute-start(f32[8,2176]{1,0:T(8,128)S(1)} %get-tuple-element.107), channel_id=1, source_target_pairs={{0,16},{16,0},{1,17},{17,1},{2,18},{18,2},{3,19},{19,3},{4,20},{20... | collective-permute-start | bytes 208904 | tf_op jit(solution)/shard_map/ppermute | solution.py:22
  105.7 5.9 %collective-permute-start.17 = (f32[8,2176]{1,0:T(8,128)S(1)}, f32[8,2176]{1,0:T(8,128)S(1)}, u32[]{:S(2)}, u32[]{:S(2)}) collective-permute-start(f32[8,2176]{1,0:T(8,128)S(1)} %get-tuple-element.80), channel_id=1, source_target_pairs={{0,16},{16,0},{1,17},{17,1},{2,18},{18,2},{3,19},{19,3},{4,20},{20... | collective-permute-start | bytes 208904 | tf_op jit(solution)/shard_map/ppermute | solution.py:22

commit v2 on v1

v2 whole, which is shorter than its diff:
```python
import functools
import math

import jax
import jax.numpy as jnp
from jax import lax
from jax.experimental import pallas as pl
from jax.experimental.pallas import tpu as pltpu
from jax.sharding import Mesh
from jax.sharding import PartitionSpec as P

Y, XL, XH, Z, C = 4, 2, 2, 8, 2
F32, BF16 = jnp.float32, jnp.bfloat16
VMEM = pl.BlockSpec(memory_space=pltpu.VMEM)
HBM = pl.BlockSpec(memory_space=pltpu.HBM)
SB, KB = 256, 256
EXT = 128


def send(x, axis, shift):
    n = lax.axis_size(axis)
    return lax.ppermute(x, axis, [(i, (i + shift) % n) for i in range(n)])


def halves(x):
    high = x.astype(BF16)
    return high, (x - high.astype(F32)).astype(BF16)


def first_pnl_kernel(
    pos, grid_in, risk, oth, b1, b2, b3, high, low, rest, posbuf, grid, rbuf, held, psem, gsem, rsem
):
    y, xl = lax.axis_index("y"), lax.axis_index("xl")
    n_inst, n_scen = risk.shape
    steps = n_inst // KB
    grid_copy = pltpu.make_async_copy(grid_in, grid, gsem)

    def fetch(q):
        part = pl.ds(pl.multiple_of(q * KB, KB), KB)
        return (
            pltpu.make_async_copy(pos.at[:, part], posbuf.at[q], psem.at[q]),
            pltpu.make_async_copy(risk.at[part, :], rbuf.at[q], rsem.at[q]),
        )

    grid_copy.start()
    for q in range(steps):
        for copy in fetch(q):
            copy.start()
    grid_copy.wait()

    blocks = [(held, 0, d, 1) for d in range(Y)]
    blocks += [(held, 1, d, e) for d in range(1, Y) for e in range(XL)]
    blocks += [(rest, 0, d, 0) for d in range(Y)] + [(rest, 1, 0, e) for e in range(XL)]
    outs = ((0, oth), (128, b1), (192, b2), (256, b3))

    def step(q, first):
        for copy in fetch(q):
            copy.wait()
        base = pl.multiple_of(q * KB, KB)
        part, at = pl.ds(base, KB), 0
        for out, k, d, e in blocks:
            if (k, d, e) == (0, 0, 0):
                at = 0
            o = lax.rem(y + d, Y) * 2 + lax.rem(xl + e, XL)
            live = [grid[o, q * (KB // 128) + i].astype(F32) for i in range(KB // 128)]
            for pair in range(2):
                row = pl.multiple_of(o * 64 + pair * 32 + k * 8, 8)
                for i in range(KB // 128):
                    lanes = slice(i * 128, i * 128 + 128)
                    x = [posbuf[q, pl.ds(row + 16 * h, 8), lanes] for h in range(2)]
                    x = jnp.concatenate(x, axis=0).astype(F32) * live[i]
                    if out is held:
                        out[at : at + 16, lanes] = x.astype(BF16)
                    else:
                        out[at : at + 16, pl.ds(pl.multiple_of(base + i * 128, 128), 128)] = x.astype(BF16)
                at += 16
        for i in range(0, KB, 128):
            rows = pl.ds(pl.multiple_of(base + i, 128), 128)
            high[rows, :], low[rows, :] = halves(rbuf[q, i : i + 128, :])
        for i in range(0, n_scen, SB):
            cols = slice(i, i + SB)
            acc = jnp.dot(held[...], high[part, cols], preferred_element_type=F32)
            acc += jnp.dot(held[...], low[part, cols], preferred_element_type=F32)
            for begin, out in outs:
                term = acc[begin : begin + out.shape[0]]
                out[:, cols] = term if first else out[:, cols] + term

    step(0, True)
    pl.loop(1, steps)(functools.partial(step, first=False))


def first_profits(positions, grid, risk):
    rows, n = risk.shape
    accounts = positions.shape[0]
    outs = [((r, n), F32) for r in (128, 64, 64, 64)] + [((rows, n), BF16)] * 2 + [((192, rows), BF16)]
    return pl.pallas_call(
        first_pnl_kernel,
        out_shape=[jax.ShapeDtypeStruct(*o) for o in outs],
        in_specs=[HBM] * 3,
        out_specs=[VMEM] * len(outs),
        scratch_shapes=[
            pltpu.VMEM((rows // KB, accounts, KB), jnp.int32),
            pltpu.SMEM(grid.shape, jnp.int32),
            pltpu.VMEM((rows // KB, KB, n), F32),
            pltpu.VMEM((320, KB), BF16),
            pltpu.SemaphoreType.DMA((rows // KB,)),
            pltpu.SemaphoreType.DMA,
            pltpu.SemaphoreType.DMA((rows // KB,)),
        ],
        compiler_params=pltpu.CompilerParams(vmem_limit_bytes=24 << 20),
        cost_estimate=pl.CostEstimate(flops=4 * 320 * rows * n, bytes_accessed=12 << 20, transcendentals=0),
    )(*(pltpu.with_memory_space_constraint(a, pltpu.HBM) for a in (positions, grid, risk)))


def rest_pnl_kernel(rest, high, low, own, b0):
    @pl.loop(0, high.shape[1] // SB)
    def _(j):
        cols = pl.ds(pl.multiple_of(j * SB, SB), SB)
        acc = jnp.dot(rest[...], high[:, cols], preferred_element_type=F32)
        acc += jnp.dot(rest[...], low[:, cols], preferred_element_type=F32)
        own[:, cols] = acc[:128]
        b0[:, cols] = acc[128:]


def rest_profits(rest, high, low):
    n = high.shape[1]
    return pl.pallas_call(
        rest_pnl_kernel,
        out_shape=[jax.ShapeDtypeStruct((r, n), F32) for r in (128, 64)],
        in_specs=[VMEM] * 3,
        out_specs=[VMEM] * 2,
        compiler_params=pltpu.CompilerParams(vmem_limit_bytes=6 << 20),
        cost_estimate=pl.CostEstimate(flops=4 * rest.size * n, bytes_accessed=12 << 20, transcendentals=0),
    )(rest, high, low)


def tails_of(softness, pieces, layout, both, put_stats):
    lane = lax.broadcasted_iota(jnp.int32, (8, EXT), 1)
    owned, at, rows = jnp.zeros((8, EXT), F32), 0, both.shape[0] // 2
    for ref, blocks in zip(pieces, layout, strict=True):
        for b, (d, e) in enumerate(blocks):
            score = ref[b * 32 : b * 32 + 32, :] * (-1.0 / softness)
            peak = jnp.max(score, axis=1, keepdims=True)
            tail = jnp.exp(score - peak)
            total = jnp.sum(tail, axis=1, keepdims=True)
            both[at : at + 32, :], both[rows + at : rows + at + 32, :] = halves(tail)
            for t in range(4):
                part = slice(t * 8, t * 8 + 8)
                put_stats(at + t * 8, jnp.where(lane < 32, peak[part], jnp.where(lane < 64, total[part], 0.0)))
                if (d, e) == (0, 0):
                    owned = jnp.where(lane == 64 + t, peak[part], owned)
                    owned = jnp.where(lane == 96 + t, total[part], owned)
            at += 32
    return owned


def block_product(both, high, low, i):
    rows = both.shape[0] // 2

    def mul(a, b):
        return lax.dot_general(a, b, (((1,), (1,)), ((), ())), preferred_element_type=F32)

    part = pl.ds(pl.multiple_of(i * SB, SB), SB)
    twice = mul(both[...], high[part, :])
    return twice[:rows] + twice[rows:] + mul(both[:rows, :], low[part, :])


def early_kernel(softness, layout, *refs):
    pieces, (high, low, out, both) = refs[: len(layout)], refs[len(layout) :]
    n_inst = high.shape[0]

    def put_stats(row, stats):
        out[row : row + 8, n_inst:] = stats

    owned = tails_of(softness, pieces, layout, both, put_stats)
    lane = lax.broadcasted_iota(jnp.int32, (8, EXT), 1)
    out[:8, n_inst:] = jnp.where(lane < 64, out[:8, n_inst:], owned)

    @pl.loop(0, n_inst // SB)
    def _(i):
        out[:, pl.ds(pl.multiple_of(i * SB, SB), SB)] = block_product(both, high, low, i)


def late_kernel(softness, layout, done_layout, *refs):
    pieces, (done, high, low, own, oth, both, full) = refs[: len(layout)], refs[len(layout) :]
    y, xl, xh, z, c = (lax.axis_index(a) for a in ("y", "xl", "xh", "z", "c"))
    n_inst = high.shape[0]
    lane = lax.broadcasted_iota(jnp.int32, (8, EXT), 1)

    def places(blocks):
        found = []
        for d, e in blocks:
            o = lax.rem(y + d, Y) * 2 + lax.rem(xl + e, XL)
            other_xh = jnp.where(o // 4 == xh, 0, 1)
            for t in range(4):
                dz = lax.rem(lax.rem(o, 4) * 2 + t // 2 + Z - z, Z)
                dc = jnp.where(c == t % 2, 0, 1)
                found.append(pl.ds(pl.multiple_of(((dc * Z + dz) * XH + other_xh) * 8, 8), 8))
        return found

    place = places(sum(layout, []))

    def put_stats(row, stats):
        full[place[row // 8], n_inst:] = stats

    tails_of(softness, pieces, layout, both, put_stats)
    for g, rows in enumerate(places(done_layout)):
        part = slice(g * 8, g * 8 + 8)
        full[rows, :n_inst] = done[part, :n_inst]
        full[rows, n_inst:] = jnp.where(lane < 64, done[part, n_inst:], 0.0)

    @pl.loop(0, n_inst // SB)
    def _(i):
        acc = block_product(both, high, low, i)
        cols = pl.ds(pl.multiple_of(i * SB, SB), SB)
        for g, rows in enumerate(place):
            full[rows, cols] = acc[g * 8 : g * 8 + 8]

    half = full.shape[0] // 2
    for out, first in ((own, 0), (oth, half)):
        for row in range(0, half, 8):
            out[row : row + 8, :] = full[first + row : first + row + 8, :]
        out[:8, n_inst:] = jnp.where(lane < 64, full[first : first + 8, n_inst:], done[:8, n_inst:])


def gradients(kernel, pieces, high, low, out_rows, scratch, done=()):
    n_inst, n_scen = high.shape
    rows = sum(p.shape[0] for p in pieces)
    return pl.pallas_call(
        kernel,
        out_shape=[jax.ShapeDtypeStruct((r, n_inst + EXT), F32) for r in out_rows],
        in_specs=[VMEM] * (len(pieces) + len(done) + 2),
        out_specs=[VMEM] * len(out_rows),
        scratch_shapes=[pltpu.VMEM((2 * rows, n_scen), BF16)] + scratch,
        compiler_params=pltpu.CompilerParams(vmem_limit_bytes=12 << 20),
        cost_estimate=pl.CostEstimate(
            flops=6 * rows * n_inst * n_scen, bytes_accessed=8 << 20, transcendentals=rows * n_scen
        ),
    )(*pieces, *done, high, low)


def merge(parts):
    peaks = [p[:, -EXT : -EXT + 1] for p in parts]
    peak = peaks[0]
    for other in peaks[1:]:
        peak = jnp.maximum(peak, other)
    total = None
    for part, own_peak in zip(parts, peaks, strict=True):
        term = part * jnp.exp(own_peak - peak)
        total = term if total is None else total + term
    lane = lax.broadcasted_iota(jnp.int32, (total.shape[0], EXT), 1)
    return total[:, :-EXT], jnp.where(lane < 32, peak, total[:, -EXT:])


def merge_owned(blocks):
    above = [pltpu.roll(b, 32, 1) for b in blocks]
    largest, peak = blocks[0], above[0]
    for b, a in zip(blocks[1:], above[1:], strict=True):
        largest, peak = jnp.maximum(largest, b), jnp.maximum(peak, a)
    total = sum(b * jnp.exp(a - peak) for b, a in zip(blocks, above, strict=True))
    lane = lax.broadcasted_iota(jnp.int32, (8, EXT), 1)
    return jnp.where(lane < 96, largest, total)


def put(out, rows, parts, owned=None):
    data, stats = merge(parts)
    out[rows, :-EXT] = data
    if owned is not None:
        lane = lax.broadcasted_iota(jnp.int32, stats.shape, 1)
        stats = jnp.where(lane < 64, stats, owned)
    out[rows, -EXT:] = stats


def call(kernel, outs, *args):
    return pl.pallas_call(
        kernel,
        out_shape=[jax.ShapeDtypeStruct(s, F32) for s in outs],
        in_specs=[VMEM] * len(args),
        out_specs=[VMEM] * len(outs),
        compiler_params=pltpu.CompilerParams(vmem_limit_bytes=4 << 20),
        cost_estimate=pl.CostEstimate(
            flops=sum(a.size for a in args), bytes_accessed=8 * sum(a.size for a in args), transcendentals=0
        ),
    )(*args)


LOW, HIGH = slice(0, 8), slice(8, 16)


def put_rows(out, *parts, owned=None):
    for rows in (LOW, HIGH):
        put(out, rows, [p[rows, :] for p in parts], owned if rows == LOW else None)


def core_kernel(own, came, *outs):
    owned = merge_owned([own[LOW, -EXT:], came[LOW, -EXT:]])
    outs[-1][...] = owned
    for d, out in enumerate(outs[:-1]):
        rows = slice(d * 16, d * 16 + 16)
        put_rows(out, own.at[rows, :], came.at[rows, :], owned=owned if d in (3, 4, 5) else None)


def next_kernel(own, came, *refs):
    out, acc = refs[-2:]
    owned = came[LOW, -EXT:]
    put_rows(out, own, came, owned=owned)
    acc[...] = merge_owned([refs[0][...], owned]) if len(refs) == 3 else owned


def last_kernel(*refs):
    kept, gone = refs[-2:]
    for group, rows in zip((refs[:5], refs[5:10]), (LOW, HIGH), strict=True):
        here, flows, accs = group[0], group[1:3], group[3:]
        owned = merge_owned([a[...] for a in accs] + [f[LOW, -EXT:] for f in flows])
        for h, out in ((LOW, kept), (HIGH, gone)):
            put(out, rows, [here[h, :]] + [f[h, :] for f in flows], owned)


def end_kernel(scenarios, kept, came, out, margin):
    values = []
    for rows in (LOW, HIGH):
        data, stats = merge([kept[rows, :], came[rows, :]])
        out[rows, :] = -data / stats[:, 32:33]
        owned = merge_owned([kept[rows, -EXT:], came[rows, -EXT:]])
        values.append(pltpu.roll(owned, 32, 1) + jnp.log(owned) - math.log(scenarios))
    values.append(jnp.zeros((EXT - 16, EXT), F32))
    columns = jnp.concatenate(values, axis=0).T[96:104, :]
    line = columns[:1]
    for t in range(1, 4):
        line += pltpu.roll(columns, 16 * t, 1)[t : t + 1]
    margin[...] = line[:, :64]


def body(positions, grid, risk):
    _, n_inst = positions.shape
    n_scen = risk.shape[1]
    softness = 8.0 * math.sqrt(n_inst * Y * XL)
    scenarios = n_scen * XH * Z * C

    oth, b1, b2, b3, high, low, remaining = first_profits(positions, grid, risk)
    x0 = send(oth, "xl", 1)
    r1, r3, r2 = send(b1, "y", 1), send(b3, "y", -1), send(b2, "y", 2)
    own, b0 = rest_profits(remaining, high, low)
    near = [own[d * 32 : d * 32 + 32] + x0[d * 32 : d * 32 + 32] for d in range(Y)]
    pair = b0 + r1 + r3 + r2
    q1, q3, q2 = (send(near[d], "y", s) for d, s in ((1, 1), (3, -1), (2, 2)))
    x1 = send(pair, "xl", 1)
    m0 = near[0] + q1 + q3 + q2
    both = pair + jnp.concatenate([x1[32:], x1[:32]])

    c3, c1, c2 = (send(m0, "y", s) for s in (1, -1, 2))
    row = jnp.concatenate([m0, c1, c2, c3])
    rest = send(row, "xl", 1)
    e3, e1, e2 = (send(both, "y", s) for s in (1, -1, 2))

    width = n_inst + EXT
    groups = (
        ((row,), [[(d, 0) for d in range(Y)]], (rest,), [[(d, 1) for d in range(Y)]]),
        ((both,), [[(0, 0), (0, 1)]], (e1, e2, e3), [[(d, 0), (d, 1)] for d in (1, 2, 3)]),
    )
    dones = []
    for pieces, layout, _, _ in groups:
        kernel = functools.partial(early_kernel, softness, layout)
        dones += gradients(kernel, pieces, high, low, [pieces[0].shape[0]], [])
    dones = lax.optimization_barrier(tuple(dones))

    ends = []
    for (_, layout, late_pieces, late_layout), done in zip(groups, dones, strict=True):
        kernel = functools.partial(late_kernel, softness, late_layout, layout[0])
        scratch = [pltpu.VMEM((256, width), F32)]
        kept, gone = gradients(kernel, late_pieces, high, low, [128, 128], scratch, [done])
        came = send(gone, "c", 1)
        *at, acc = call(core_kernel, [(16, width)] * Z + [(8, EXT)], kept, came)
        up, down = ((4, 3, 2, 1), (5, 6, 7)) if not ends else ((3, 2, 1), (4, 5, 6, 7))
        flows, accs = [], []
        for hops, shift in ((up, 1), (down, -1)):
            kind = [acc] if len(hops) == 4 else []
            flow = send(at[hops[0]], "z", shift)
            for d in hops[1:]:
                flow, *kind = call(next_kernel, [(16, width), (8, EXT)], at[d], flow, *kind)
                flow = send(flow, "z", shift)
            flows.append(flow)
            accs += kind
        ends += [at[0], *flows, *accs]
    kept, gone = call(last_kernel, [(16, width)] * 2, *ends)
    last = functools.partial(end_kernel, scenarios)
    gradient, margin = call(last, [(16, n_inst), (1, 64)], kept, send(gone, "xh", 1))
    margin = margin.reshape(64)
    return margin, gradient


def solution(mesh):
    torus = Mesh(mesh.devices.reshape(Y, XL, XH, Z, C), ("y", "xl", "xh", "z", "c"))
    inst, scen = ("y", "xl"), ("xh", "z", "c")
    return jax.shard_map(
        body,
        mesh=torus,
        in_specs=(P(None, inst), P(None, inst), P(inst, scen)),
        out_specs=(P(inst), P(scen, inst)),
        check_vma=False,
    )
```

time: 113 us -> 109 us (0.965)
  starting transfers between devices: 57.7 us -> 46.7 us
  Pallas kernels: 23.8 us -> 29.2 us
  waiting for transfers between devices: 29.8 us -> 31.6 us
    ppermute x35 -> x32, starting transfers between devices: 57.7 us -> 46.7 us  [send(): return lax.ppermute(x, axis, [(i, (i + shift) % n) for i in range(n)])]
    pallas_call x3 -> x6, Pallas kernels: 21.7 us -> 26.8 us  [the longest x4 16.9 us: gradients(): pl.pallas_call(kernel, out_shape=[jax.ShapeDtypeStruct((r, n_inst + EXT),...]
    ppermute x35 -> x32, waiting for transfers between devices: 29.8 us -> 31.6 us  [send(): return lax.ppermute(x, axis, [(i, (i + shift) % n) for i in range(n)])]
    pallas_call x11 -> x14, Pallas kernels: 2.14 us -> 2.42 us  [call(): pl.pallas_call(kernel, out_shape=[jax.ShapeDtypeStruct(s, F32) for s in o...]
  transfers between devices with their start and end apart: 35 -> 32, of which waited for: 18 -> 16; matrix products, arithmetic and copies ran while one was open for 0% -> 0% of each run, Pallas kernels for 12% -> 19%
where the time goes in v2:
time: 109 us
  starting transfers between devices  46.7 us (43%)
  waiting for transfers between devices  31.6 us (29%)
  Pallas kernels  29.2 us (27%)
    ppermute x32, starting transfers between devices, send(): return lax.ppermute(x, axis, [(i, (i + shift) % n) for i in range(n)])  46.7 us
    ppermute x32, waiting for transfers between devices, send(): return lax.ppermute(x, axis, [(i, (i + shift) % n) for i in range(n)])  31.6 us
    pallas_call x4, Pallas kernels, gradients(): pl.pallas_call(kernel, out_shape=[jax.ShapeDtypeStruct((r, n_inst + EXT),...  16.9 us
    pallas_call x1, Pallas kernels, first_profits(): pl.pallas_call(first_pnl_kernel, out_shape=[jax.ShapeDtypeStruct(*o) for...  7.4 us
    pallas_call x1, Pallas kernels, rest_profits(): pl.pallas_call(rest_pnl_kernel, out_shape=[jax.ShapeDtypeStruct((r, n), F...  2.47 us
    pallas_call x14, Pallas kernels, call(): pl.pallas_call(kernel, out_shape=[jax.ShapeDtypeStruct(s, F32) for s in o...  2.42 us
  transfers between devices with their start and end apart: 32, of which 16 were waited for; matrix products, arithmetic and copies ran while one was open for 0% of the time, Pallas kernels for 19%

profile of v2, /device:TPU:2, one launch (start us, length us, event | category | flops | bytes accessed | tf_op | source)
XLA Modules:
  0.0 108.7 jit_solution(10589862545075265657)
XLA Ops:
  0.6 7.4 %shard_map.50 = (f32[128,1024]{1,0:T(8,128)S(1)}, f32[64,1024]{1,0:T(8,128)S(1)}, f32[64,1024]{1,0:T(8,128)S(1)}, f32[64,1024]{1,0:T(8,128)S(1)}, bf16[2048,1024...) custom-call(s32[512,2048]{1,0:T(8,128)} %pos.1, s32[8,16]{1,0:T(8,128)} %grid_in.1, ...), custom_call_target="tpu_custom_call" | custom-call | flops 2684354560 | bytes 12582912 | tf_op jit(solution)/shard_map/pallas_call | solution.py:96
  8.0 2.3 %collective-permute-start = (f32[128,1024]{1,0:T(8,128)S(1)}, f32[128,1024]{1,0:T(8,128)S(1)}, u32[]{:S(2)}, u32[]{:S(2)}) collective-permute-start(f32[128,1024]{1,0:T(8,128)S(1)} %get-tuple-element.63), channel_id=1, source_target_pairs={{0,32},{32,0},{1,33},{33,1},{2,34},{34,2},{3,35},{35,3},{4,36},{36... | collective-permute-start | bytes 1572872 | tf_op jit(solution)/shard_map/ppermute | solution.py:22
  10.4 1.5 %collective-permute-start.10 = (f32[64,1024]{1,0:T(8,128)S(1)}, f32[64,1024]{1,0:T(8,128)S(1)}, u32[]{:S(2)}, u32[]{:S(2)}) collective-permute-start(f32[64,1024]{1,0:T(8,128)S(1)} %get-tuple-element.67), channel_id=1, source_target_pairs={{0,128},{64,192},{128,0},{192,64},{1,129},{65,193},{129,1},{193,65... | collective-permute-start | bytes 786440 | tf_op jit(solution)/shard_map/ppermute | solution.py:22
  11.8 1.1 collective-permute-start.9
  12.9 1.0 collective-permute-start.8
  13.9 2.5 %shard_map.51 = (f32[128,1024]{1,0:T(8,128)S(1)}, f32[64,1024]{1,0:T(8,128)S(1)}) custom-call(bf16[192,2048]{1,0:T(8,128)(2,1)S(1)} %get-tuple-element.59.rest, bf16[2048,1024]{1,0:T(8,128)(2,1)S(1)} %get-tuple-element.60.high.refs_1_.refs_2_.refs_4_, bf16[2048,1024]{1,0:T(8,128)(2,1)S(1)} %get-tuple-element.61.low.refs_2_.refs_3_.refs_5_), custom_call_target="tpu_custom_call" | custom-call | flops 1610612736 | bytes 12582912 | tf_op jit(solution)/shard_map/pallas_call | solution.py:127
  16.4 5.5 %collective-permute-done = f32[128,1024]{1,0:T(8,128)S(1)} collective-permute-done((f32[128,1024]{1,0:T(8,128)S(1)}, f32[128,1024]{1,0:T(8,128)S(1)}, u32[]{:S(2)}, u32[]{:S(2)}) %collective-permute-start) | collective-permute-done | bytes 524320 | tf_op jit(solution)/shard_map/ppermute | solution.py:22
  21.9 3.3 %collective-permute-start.3 = (f32[32,1024]{1,0:T(8,128)S(1)}, f32[32,1024]{1,0:T(8,128)S(1)}, u32[]{:S(2)}, u32[]{:S(2)}) collective-permute-start(f32[32,1024]{1,0:T(8,128)S(1)} %get-tuple-element.117), channel_id=1, source_target_pairs={{0,128},{64,192},{128,0},{192,64},{1,129},{65,193},{129,1},{193,65... | collective-permute-start | bytes 393224 | tf_op jit(solution)/shard_map/ppermute | solution.py:22
  25.1 1.1 collective-permute-start.2
  26.2 1.0 collective-permute-start.1
  27.2 0.6 collective-permute-start.11
  27.9 1.9 %collective-permute-done.3 = f32[32,1024]{1,0:T(8,128)S(1)} collective-permute-done((f32[32,1024]{1,0:T(8,128)S(1)}, f32[32,1024]{1,0:T(8,128)S(1)}, u32[]{:S(2)}, u32[]{:S(2)}) %collective-permute-start.3) | collective-permute-done | bytes 131104 | tf_op jit(solution)/shard_map/ppermute | solution.py:22
  29.7 1.2 %collective-permute-done.2 = f32[32,1024]{1,0:T(8,128)S(1)} collective-permute-done((f32[32,1024]{1,0:T(8,128)S(1)}, f32[32,1024]{1,0:T(8,128)S(1)}, u32[]{:S(2)}, u32[]{:S(2)}) %collective-permute-start.2) | collective-permute-done | bytes 131104 | tf_op jit(solution)/shard_map/ppermute | solution.py:22
  30.9 1.4 %collective-permute-done.1 = f32[32,1024]{1,0:T(8,128)S(1)} collective-permute-done((f32[32,1024]{1,0:T(8,128)S(1)}, f32[32,1024]{1,0:T(8,128)S(1)}, u32[]{:S(2)}, u32[]{:S(2)}) %collective-permute-start.1) | collective-permute-done | bytes 131104 | tf_op jit(solution)/shard_map/ppermute | solution.py:22
  32.5 2.7 %collective-permute-start.5 = (f32[32,1024]{1,0:T(8,128)S(1)}, f32[32,1024]{1,0:T(8,128)S(1)}, u32[]{:S(2)}, u32[]{:S(2)}) collective-permute-start(f32[32,1024]{1,0:T(8,128)S(1)} %fusion.2), channel_id=1, source_target_pairs={{0,128},{64,192},{128,0},{192,64},{1,129},{65,193},{129,1},{193,65... | collective-permute-start | bytes 393224 | tf_op jit(solution)/shard_map/ppermute | solution.py:22
  35.2 1.3 %collective-permute-start.4 = (f32[32,1024]{1,0:T(8,128)S(1)}, f32[32,1024]{1,0:T(8,128)S(1)}, u32[]{:S(2)}, u32[]{:S(2)}) collective-permute-start(f32[32,1024]{1,0:T(8,128)S(1)} %fusion.2), channel_id=1, source_target_pairs={{0,192},{64,0},{128,64},{192,128},{1,193},{65,1},{129,65},{193,129... | collective-permute-start | bytes 393224 | tf_op jit(solution)/shard_map/ppermute | solution.py:22
  36.6 4.1 %collective-permute-done.6 = f32[32,1024]{1,0:T(8,128)S(1)} collective-permute-done((f32[32,1024]{1,0:T(8,128)S(1)}, f32[32,1024]{1,0:T(8,128)S(1)}, u32[]{:S(2)}, u32[]{:S(2)}) %collective-permute-start.6) | collective-permute-done | bytes 131104 | tf_op jit(solution)/shard_map/ppermute | solution.py:22
  40.7 0.2 collective-permute-done.4
  41.0 0.6 collective-permute-start.7
  41.6 2.8 %collective-permute-start.20 = (f32[64,1024]{1,0:T(8,128)S(1)}, f32[64,1024]{1,0:T(8,128)S(1)}, u32[]{:S(2)}, u32[]{:S(2)}) collective-permute-start(f32[64,1024]{1,0:T(8,128)S(1)} %maximum_add_fusion.refs_0_), channel_id=1, source_target_pairs={{0,192},{64,0},{128,64},{192,128},{1,193},{65,1},{129,65},{193,129... | collective-permute-start | bytes 786440 | tf_op jit(solution)/shard_map/ppermute | solution.py:22
  44.4 0.8 collective-permute-start.21
  45.1 0.2 collective-permute-start.22
  45.3 3.9 %shard_map.53.refs_3_ = f32[64,2176]{1,0:T(8,128)S(1)} custom-call(f32[64,1024]{1,0:T(8,128)S(1)} %maximum_add_fusion.refs_0_, bf16[2048,1024]{1,0:T(8,128)(2,1)S(1)} %get-tuple-element.60.high.refs_1_.refs_2_.refs_4_, bf16[2048,1024]{1,0:T(8,128)(2,1)S(1)} %get-tuple-element.61.low.refs_2_.refs_3_.refs_5_), custom_call_target="tpu_custom_call" | custom-call | flops 805306368 | bytes 8388608 | tf_op jit(solution)/shard_map/pallas_call | solution.py:229
  49.2 3.9 %shard_map.52.refs_1_ = f32[128,2176]{1,0:T(8,128)S(1)} custom-call(f32[128,1024]{1,0:T(8,128)S(1)} %pad_maximum_fusion.refs_0_, bf16[2048,1024]{1,0:T(8,128)(2,1)S(1)} %get-tuple-element.60.high.refs_1_.refs_2_.refs_4_, bf16[2048,1024]{1,0:T(8,128)(2,1)S(1)} %get-tuple-element.61.low.refs_2_.refs_3_.refs_5_), custom_call_target="tpu_custom_call" | custom-call | flops 1610612736 | bytes 8388608 | tf_op jit(solution)/shard_map/pallas_call | solution.py:229
  53.1 2.4 %collective-permute-done.22.refs_2_ = f32[64,1024]{1,0:T(8,128)S(1)} collective-permute-done((f32[64,1024]{1,0:T(8,128)S(1)}, f32[64,1024]{1,0:T(8,128)S(1)}, u32[]{:S(2)}, u32[]{:S(2)}) %collective-permute-start.22) | collective-permute-done | bytes 262176 | tf_op jit(solution)/shard_map/ppermute | solution.py:22
  55.5 5.0 %shard_map.61 = (f32[128,2176]{1,0:T(8,128)S(1)}, f32[128,2176]{1,0:T(8,128)S(1)}) custom-call(f32[64,1024]{1,0:T(8,128)S(1)} %collective-permute-done.20.refs_0_, f32[64,1024]{1,0:T(8,128)S(1)} %collective-permute-done.21.refs_1_, f32[64,1024]{1,0:T(8,128)S(1)} %collective-permute-done.22.refs_2_, f32[64,2176]{1,0:T(8,128)S(1)} %shard_map.53.refs_3_, ...), custom_call_target="tpu_custom_call" | custom-call | flops 2415919104 | bytes 8388608 | tf_op jit(solution)/shard_map/pallas_call | solution.py:229
  60.5 0.1 collective-permute-start.23
  60.6 4.2 %shard_map.54 = (f32[128,2176]{1,0:T(8,128)S(1)}, f32[128,2176]{1,0:T(8,128)S(1)}) custom-call(f32[128,1024]{1,0:T(8,128)S(1)} %collective-permute-done.7.refs_0_, f32[128,2176]{1,0:T(8,128)S(1)} %shard_map.52.refs_1_, bf16[2048,1024]{1,0:T(8,128)(2,1)S(1)} %get-tuple-element.60.high.refs_1_.refs_2_.refs_4_, ...), custom_call_target="tpu_custom_call" | custom-call | flops 1610612736 | bytes 8388608 | tf_op jit(solution)/shard_map/pallas_call | solution.py:229
  64.8 0.6 collective-permute-start.12
  65.4 0.2 shard_map.62
  65.6 6.1 %collective-permute-start.27 = (f32[16,2176]{1,0:T(8,128)S(1)}, f32[16,2176]{1,0:T(8,128)S(1)}, u32[]{:S(2)}, u32[]{:S(2)}) collective-permute-start(f32[16,2176]{1,0:T(8,128)S(1)} %get-tuple-element.103), channel_id=1, source_target_pairs={{0,14},{2,0},{4,2},{6,4},{8,6},{10,8},{12,10},{14,12},{1,15},{3,1}... | collective-permute-start | bytes 417800 | tf_op jit(solution)/shard_map/ppermute | solution.py:22
  71.7 0.2 shard_map.55
  72.1 2.7 %collective-permute-done.27.came = f32[16,2176]{1,0:T(8,128)S(1)} collective-permute-done((f32[16,2176]{1,0:T(8,128)S(1)}, f32[16,2176]{1,0:T(8,128)S(1)}, u32[]{:S(2)}, u32[]{:S(2)}) %collective-permute-start.27) | collective-permute-done | bytes 139296 | tf_op jit(solution)/shard_map/ppermute | solution.py:22
  74.8 0.1 shard_map.65
  74.9 3.8 %collective-permute-start.28 = (f32[16,2176]{1,0:T(8,128)S(1)}, f32[16,2176]{1,0:T(8,128)S(1)}, u32[]{:S(2)}, u32[]{:S(2)}) collective-permute-start(f32[16,2176]{1,0:T(8,128)S(1)} %get-tuple-element.105), channel_id=1, source_target_pairs={{0,14},{2,0},{4,2},{6,4},{8,6},{10,8},{12,10},{14,12},{1,15},{3,1}... | collective-permute-start | bytes 417800 | tf_op jit(solution)/shard_map/ppermute | solution.py:22
  78.7 0.1 collective-permute-start.17
  78.8 1.0 collective-permute-done.13.came
  79.7 0.1 shard_map.56
  79.8 1.0 collective-permute-start.14
  80.9 0.6 collective-permute-done.24.came
  81.5 0.1 shard_map.63
  81.7 0.7 collective-permute-done.28.came
  82.4 0.1 shard_map.66
  82.5 3.8 %collective-permute-start.29 = (f32[16,2176]{1,0:T(8,128)S(1)}, f32[16,2176]{1,0:T(8,128)S(1)}, u32[]{:S(2)}, u32[]{:S(2)}) collective-permute-start(f32[16,2176]{1,0:T(8,128)S(1)} %get-tuple-element.107), channel_id=1, source_target_pairs={{0,14},{2,0},{4,2},{6,4},{8,6},{10,8},{12,10},{14,12},{1,15},{3,1}... | collective-permute-start | bytes 417800 | tf_op jit(solution)/shard_map/ppermute | solution.py:22
  86.3 0.1 shard_map.59
  86.4 1.5 %collective-permute-start.18 = (f32[16,2176]{1,0:T(8,128)S(1)}, f32[16,2176]{1,0:T(8,128)S(1)}, u32[]{:S(2)}, u32[]{:S(2)}) collective-permute-start(f32[16,2176]{1,0:T(8,128)S(1)} %get-tuple-element.85), channel_id=1, source_target_pairs={{0,14},{2,0},{4,2},{6,4},{8,6},{10,8},{12,10},{14,12},{1,15},{3,1}... | collective-permute-start | bytes 417800 | tf_op jit(solution)/shard_map/ppermute | solution.py:22
  87.9 0.1 shard_map.57
  88.0 0.7 collective-permute-start.15
  88.7 0.2 collective-permute-done.25.came
  88.8 0.1 shard_map.64
  88.9 0.3 collective-permute-start.26
  89.3 0.1 shard_map.67
  89.4 3.7 %collective-permute-start.30 = (f32[16,2176]{1,0:T(8,128)S(1)}, f32[16,2176]{1,0:T(8,128)S(1)}, u32[]{:S(2)}, u32[]{:S(2)}) collective-permute-start(f32[16,2176]{1,0:T(8,128)S(1)} %get-tuple-element.109), channel_id=1, source_target_pairs={{0,14},{2,0},{4,2},{6,4},{8,6},{10,8},{12,10},{14,12},{1,15},{3,1}... | collective-permute-start | bytes 417800 | tf_op jit(solution)/shard_map/ppermute | solution.py:22
  93.1 0.1 shard_map.60
  93.2 1.4 %collective-permute-start.19 = (f32[16,2176]{1,0:T(8,128)S(1)}, f32[16,2176]{1,0:T(8,128)S(1)}, u32[]{:S(2)}, u32[]{:S(2)}) collective-permute-start(f32[16,2176]{1,0:T(8,128)S(1)} %get-tuple-element.87), channel_id=1, source_target_pairs={{0,14},{2,0},{4,2},{6,4},{8,6},{10,8},{12,10},{14,12},{1,15},{3,1}... | collective-permute-start | bytes 417800 | tf_op jit(solution)/shard_map/ppermute | solution.py:22
  94.6 0.1 shard_map.58
  94.7 0.8 collective-permute-start.16
  95.4 0.5 collective-permute-done.26.refs_6_
  95.9 2.4 %collective-permute-done.19.refs_2_ = f32[16,2176]{1,0:T(8,128)S(1)} collective-permute-done((f32[16,2176]{1,0:T(8,128)S(1)}, f32[16,2176]{1,0:T(8,128)S(1)}, u32[]{:S(2)}, u32[]{:S(2)}) %collective-permute-start.19) | collective-permute-done | bytes 139296 | tf_op jit(solution)/shard_map/ppermute | solution.py:22
  98.3 2.7 %collective-permute-done.16.refs_1_ = f32[16,2176]{1,0:T(8,128)S(1)} collective-permute-done((f32[16,2176]{1,0:T(8,128)S(1)}, f32[16,2176]{1,0:T(8,128)S(1)}, u32[]{:S(2)}, u32[]{:S(2)}) %collective-permute-start.16) | collective-permute-done | bytes 139296 | tf_op jit(solution)/shard_map/ppermute | solution.py:22
  101.0 0.1 shard_map.68
  101.1 2.5 %collective-permute-start.31 = (f32[16,2176]{1,0:T(8,128)S(1)}, f32[16,2176]{1,0:T(8,128)S(1)}, u32[]{:S(2)}, u32[]{:S(2)}) collective-permute-start(f32[16,2176]{1,0:T(8,128)S(1)} %get-tuple-element.113), channel_id=1, source_target_pairs={{0,16},{16,0},{1,17},{17,1},{2,18},{18,2},{3,19},{19,3},{4,20},{20... | collective-permute-start | bytes 417800 | tf_op jit(solution)/shard_map/ppermute | solution.py:22
  103.7 4.1 %collective-permute-done.31.came = f32[16,2176]{1,0:T(8,128)S(1)} collective-permute-done((f32[16,2176]{1,0:T(8,128)S(1)}, f32[16,2176]{1,0:T(8,128)S(1)}, u32[]{:S(2)}, u32[]{:S(2)}) %collective-permute-start.31) | collective-permute-done | bytes 139296 | tf_op jit(solution)/shard_map/ppermute | solution.py:22
  107.8 0.9 shard_map.69
  (26 shorter events, 0.6 us)
Async XLA Ops:
  8.0 13.8 %collective-permute-start = (f32[128,1024]{1,0:T(8,128)S(1)}, f32[128,1024]{1,0:T(8,128)S(1)}, u32[]{:S(2)}, u32[]{:S(2)}) collective-permute-start(f32[128,1024]{1,0:T(8,128)S(1)} %get-tuple-element.63), channel_id=1, source_target_pairs={{0,32},{32,0},{1,33},{33,1},{2,34},{34,2},{3,35},{35,3},{4,36},{36... | collective-permute-start | bytes 1572872 | tf_op jit(solution)/shard_map/ppermute | solution.py:22
  10.4 15.8 %collective-permute-start.10 = (f32[64,1024]{1,0:T(8,128)S(1)}, f32[64,1024]{1,0:T(8,128)S(1)}, u32[]{:S(2)}, u32[]{:S(2)}) collective-permute-start(f32[64,1024]{1,0:T(8,128)S(1)} %get-tuple-element.67), channel_id=1, source_target_pairs={{0,128},{64,192},{128,0},{192,64},{1,129},{65,193},{129,1},{193,65... | collective-permute-start | bytes 786440 | tf_op jit(solution)/shard_map/ppermute | solution.py:22
  11.8 15.3 %collective-permute-start.9 = (f32[64,1024]{1,0:T(8,128)S(1)}, f32[64,1024]{1,0:T(8,128)S(1)}, u32[]{:S(2)}, u32[]{:S(2)}) collective-permute-start(f32[64,1024]{1,0:T(8,128)S(1)} %get-tuple-element.66), channel_id=1, source_target_pairs={{0,192},{64,0},{128,64},{192,128},{1,193},{65,1},{129,65},{193,129... | collective-permute-start | bytes 786440 | tf_op jit(solution)/shard_map/ppermute | solution.py:22
  12.9 14.2 %collective-permute-start.8 = (f32[64,1024]{1,0:T(8,128)S(1)}, f32[64,1024]{1,0:T(8,128)S(1)}, u32[]{:S(2)}, u32[]{:S(2)}) collective-permute-start(f32[64,1024]{1,0:T(8,128)S(1)} %get-tuple-element.65), channel_id=1, source_target_pairs={{0,64},{64,128},{128,192},{192,0},{1,65},{65,129},{129,193},{193,1... | collective-permute-start | bytes 786440 | tf_op jit(solution)/shard_map/ppermute | solution.py:22
  21.9 7.9 %collective-permute-start.3 = (f32[32,1024]{1,0:T(8,128)S(1)}, f32[32,1024]{1,0:T(8,128)S(1)}, u32[]{:S(2)}, u32[]{:S(2)}) collective-permute-start(f32[32,1024]{1,0:T(8,128)S(1)} %get-tuple-element.117), channel_id=1, source_target_pairs={{0,128},{64,192},{128,0},{192,64},{1,129},{65,193},{129,1},{193,65... | collective-permute-start | bytes 393224 | tf_op jit(solution)/shard_map/ppermute | solution.py:22
  25.1 5.8 %collective-permute-start.2 = (f32[32,1024]{1,0:T(8,128)S(1)}, f32[32,1024]{1,0:T(8,128)S(1)}, u32[]{:S(2)}, u32[]{:S(2)}) collective-permute-start(f32[32,1024]{1,0:T(8,128)S(1)} %get-tuple-element.118), channel_id=1, source_target_pairs={{0,192},{64,0},{128,64},{192,128},{1,193},{65,1},{129,65},{193,129... | collective-permute-start | bytes 393224 | tf_op jit(solution)/shard_map/ppermute | solution.py:22
  26.2 6.2 %collective-permute-start.1 = (f32[32,1024]{1,0:T(8,128)S(1)}, f32[32,1024]{1,0:T(8,128)S(1)}, u32[]{:S(2)}, u32[]{:S(2)}) collective-permute-start(f32[32,1024]{1,0:T(8,128)S(1)} %get-tuple-element.116), channel_id=1, source_target_pairs={{0,64},{64,128},{128,192},{192,0},{1,65},{65,129},{129,193},{193,1... | collective-permute-start | bytes 393224 | tf_op jit(solution)/shard_map/ppermute | solution.py:22
  27.2 9.3 %collective-permute-start.11 = (f32[64,1024]{1,0:T(8,128)S(1)}, f32[64,1024]{1,0:T(8,128)S(1)}, u32[]{:S(2)}, u32[]{:S(2)}) collective-permute-start(f32[64,1024]{1,0:T(8,128)S(1)} %add_add_fusion), channel_id=1, source_target_pairs={{0,32},{32,0},{1,33},{33,1},{2,34},{34,2},{3,35},{35,3},{4,36},{36... | collective-permute-start | bytes 786440 | tf_op jit(solution)/shard_map/ppermute | solution.py:22
  32.4 8.3 %collective-permute-start.6 = (f32[32,1024]{1,0:T(8,128)S(1)}, f32[32,1024]{1,0:T(8,128)S(1)}, u32[]{:S(2)}, u32[]{:S(2)}) collective-permute-start(f32[32,1024]{1,0:T(8,128)S(1)} %fusion.2), channel_id=1, source_target_pairs={{0,64},{64,128},{128,192},{192,0},{1,65},{65,129},{129,193},{193,1... | collective-permute-start | bytes 393224 | tf_op jit(solution)/shard_map/ppermute | solution.py:22
  32.5 8.2 %collective-permute-start.5 = (f32[32,1024]{1,0:T(8,128)S(1)}, f32[32,1024]{1,0:T(8,128)S(1)}, u32[]{:S(2)}, u32[]{:S(2)}) collective-permute-start(f32[32,1024]{1,0:T(8,128)S(1)} %fusion.2), channel_id=1, source_target_pairs={{0,128},{64,192},{128,0},{192,64},{1,129},{65,193},{129,1},{193,65... | collective-permute-start | bytes 393224 | tf_op jit(solution)/shard_map/ppermute | solution.py:22
  35.2 5.7 %collective-permute-start.4 = (f32[32,1024]{1,0:T(8,128)S(1)}, f32[32,1024]{1,0:T(8,128)S(1)}, u32[]{:S(2)}, u32[]{:S(2)}) collective-permute-start(f32[32,1024]{1,0:T(8,128)S(1)} %fusion.2), channel_id=1, source_target_pairs={{0,192},{64,0},{128,64},{192,128},{1,193},{65,1},{129,65},{193,129... | collective-permute-start | bytes 393224 | tf_op jit(solution)/shard_map/ppermute | solution.py:22
  41.0 19.6 %collective-permute-start.7 = (f32[128,1024]{1,0:T(8,128)S(1)}, f32[128,1024]{1,0:T(8,128)S(1)}, u32[]{:S(2)}, u32[]{:S(2)}) collective-permute-start(f32[128,1024]{1,0:T(8,128)S(1)} %pad_maximum_fusion.refs_0_), channel_id=1, source_target_pairs={{0,32},{32,0},{1,33},{33,1},{2,34},{34,2},{3,35},{35,3},{4,36},{36... | collective-permute-start | bytes 1572872 | tf_op jit(solution)/shard_map/ppermute | solution.py:22
  41.6 11.5 %collective-permute-start.20 = (f32[64,1024]{1,0:T(8,128)S(1)}, f32[64,1024]{1,0:T(8,128)S(1)}, u32[]{:S(2)}, u32[]{:S(2)}) collective-permute-start(f32[64,1024]{1,0:T(8,128)S(1)} %maximum_add_fusion.refs_0_), channel_id=1, source_target_pairs={{0,192},{64,0},{128,64},{192,128},{1,193},{65,1},{129,65},{193,129... | collective-permute-start | bytes 786440 | tf_op jit(solution)/shard_map/ppermute | solution.py:22
  44.4 8.7 %collective-permute-start.21 = (f32[64,1024]{1,0:T(8,128)S(1)}, f32[64,1024]{1,0:T(8,128)S(1)}, u32[]{:S(2)}, u32[]{:S(2)}) collective-permute-start(f32[64,1024]{1,0:T(8,128)S(1)} %maximum_add_fusion.refs_0_), channel_id=1, source_target_pairs={{0,128},{64,192},{128,0},{192,64},{1,129},{65,193},{129,1},{193,65... | collective-permute-start | bytes 786440 | tf_op jit(solution)/shard_map/ppermute | solution.py:22
  45.1 10.4 %collective-permute-start.22 = (f32[64,1024]{1,0:T(8,128)S(1)}, f32[64,1024]{1,0:T(8,128)S(1)}, u32[]{:S(2)}, u32[]{:S(2)}) collective-permute-start(f32[64,1024]{1,0:T(8,128)S(1)} %maximum_add_fusion.refs_0_), channel_id=1, source_target_pairs={{0,64},{64,128},{128,192},{192,0},{1,65},{65,129},{129,193},{193,1... | collective-permute-start | bytes 786440 | tf_op jit(solution)/shard_map/ppermute | solution.py:22
  60.5 4.9 %collective-permute-start.23 = (f32[128,2176]{1,0:T(8,128)S(1)}, f32[128,2176]{1,0:T(8,128)S(1)}, u32[]{:S(2)}, u32[]{:S(2)}) collective-permute-start(f32[128,2176]{1,0:T(8,128)S(1)} %get-tuple-element.92), channel_id=1, source_target_pairs={{0,1},{1,0},{2,3},{3,2},{4,5},{5,4},{6,7},{7,6},{8,9},{9,8},{10,11... | collective-permute-start | bytes 3342344 | tf_op jit(solution)/shard_map/ppermute | solution.py:22
  64.8 6.9 %collective-permute-start.12 = (f32[128,2176]{1,0:T(8,128)S(1)}, f32[128,2176]{1,0:T(8,128)S(1)}, u32[]{:S(2)}, u32[]{:S(2)}) collective-permute-start(f32[128,2176]{1,0:T(8,128)S(1)} %get-tuple-element.70), channel_id=1, source_target_pairs={{0,1},{1,0},{2,3},{3,2},{4,5},{5,4},{6,7},{7,6},{8,9},{9,8},{10,11... | collective-permute-start | bytes 3342344 | tf_op jit(solution)/shard_map/ppermute | solution.py:22
  65.6 9.2 %collective-permute-start.27 = (f32[16,2176]{1,0:T(8,128)S(1)}, f32[16,2176]{1,0:T(8,128)S(1)}, u32[]{:S(2)}, u32[]{:S(2)}) collective-permute-start(f32[16,2176]{1,0:T(8,128)S(1)} %get-tuple-element.103), channel_id=1, source_target_pairs={{0,14},{2,0},{4,2},{6,4},{8,6},{10,8},{12,10},{14,12},{1,15},{3,1}... | collective-permute-start | bytes 417800 | tf_op jit(solution)/shard_map/ppermute | solution.py:22
  71.9 7.8 %collective-permute-start.13 = (f32[16,2176]{1,0:T(8,128)S(1)}, f32[16,2176]{1,0:T(8,128)S(1)}, u32[]{:S(2)}, u32[]{:S(2)}) collective-permute-start(f32[16,2176]{1,0:T(8,128)S(1)} %get-tuple-element.75), channel_id=1, source_target_pairs={{0,2},{2,4},{4,6},{6,8},{8,10},{10,12},{12,14},{14,0},{1,3},{3,5},... | collective-permute-start | bytes 417800 | tf_op jit(solution)/shard_map/ppermute | solution.py:22
  72.0 9.5 %collective-permute-start.24 = (f32[16,2176]{1,0:T(8,128)S(1)}, f32[16,2176]{1,0:T(8,128)S(1)}, u32[]{:S(2)}, u32[]{:S(2)}) collective-permute-start(f32[16,2176]{1,0:T(8,128)S(1)} %get-tuple-element.96), channel_id=1, source_target_pairs={{0,2},{2,4},{4,6},{6,8},{8,10},{10,12},{12,14},{14,0},{1,3},{3,5},... | collective-permute-start | bytes 417800 | tf_op jit(solution)/shard_map/ppermute | solution.py:22
  74.9 7.5 %collective-permute-start.28 = (f32[16,2176]{1,0:T(8,128)S(1)}, f32[16,2176]{1,0:T(8,128)S(1)}, u32[]{:S(2)}, u32[]{:S(2)}) collective-permute-start(f32[16,2176]{1,0:T(8,128)S(1)} %get-tuple-element.105), channel_id=1, source_target_pairs={{0,14},{2,0},{4,2},{6,4},{8,6},{10,8},{12,10},{14,12},{1,15},{3,1}... | collective-permute-start | bytes 417800 | tf_op jit(solution)/shard_map/ppermute | solution.py:22
  78.7 7.6 %collective-permute-start.17 = (f32[16,2176]{1,0:T(8,128)S(1)}, f32[16,2176]{1,0:T(8,128)S(1)}, u32[]{:S(2)}, u32[]{:S(2)}) collective-permute-start(f32[16,2176]{1,0:T(8,128)S(1)} %get-tuple-element.84), channel_id=1, source_target_pairs={{0,14},{2,0},{4,2},{6,4},{8,6},{10,8},{12,10},{14,12},{1,15},{3,1}... | collective-permute-start | bytes 417800 | tf_op jit(solution)/shard_map/ppermute | solution.py:22
  79.8 8.0 %collective-permute-start.14 = (f32[16,2176]{1,0:T(8,128)S(1)}, f32[16,2176]{1,0:T(8,128)S(1)}, u32[]{:S(2)}, u32[]{:S(2)}) collective-permute-start(f32[16,2176]{1,0:T(8,128)S(1)} %get-tuple-element.77), channel_id=1, source_target_pairs={{0,2},{2,4},{4,6},{6,8},{8,10},{10,12},{12,14},{14,0},{1,3},{3,5},... | collective-permute-start | bytes 417800 | tf_op jit(solution)/shard_map/ppermute | solution.py:22
  81.6 7.2 %collective-permute-start.25 = (f32[16,2176]{1,0:T(8,128)S(1)}, f32[16,2176]{1,0:T(8,128)S(1)}, u32[]{:S(2)}, u32[]{:S(2)}) collective-permute-start(f32[16,2176]{1,0:T(8,128)S(1)} %get-tuple-element.97), channel_id=1, source_target_pairs={{0,2},{2,4},{4,6},{6,8},{8,10},{10,12},{12,14},{14,0},{1,3},{3,5},... | collective-permute-start | bytes 417800 | tf_op jit(solution)/shard_map/ppermute | solution.py:22
  82.5 6.7 %collective-permute-start.29 = (f32[16,2176]{1,0:T(8,128)S(1)}, f32[16,2176]{1,0:T(8,128)S(1)}, u32[]{:S(2)}, u32[]{:S(2)}) collective-permute-start(f32[16,2176]{1,0:T(8,128)S(1)} %get-tuple-element.107), channel_id=1, source_target_pairs={{0,14},{2,0},{4,2},{6,4},{8,6},{10,8},{12,10},{14,12},{1,15},{3,1}... | collective-permute-start | bytes 417800 | tf_op jit(solution)/shard_map/ppermute | solution.py:22
  86.4 6.7 %collective-permute-start.18 = (f32[16,2176]{1,0:T(8,128)S(1)}, f32[16,2176]{1,0:T(8,128)S(1)}, u32[]{:S(2)}, u32[]{:S(2)}) collective-permute-start(f32[16,2176]{1,0:T(8,128)S(1)} %get-tuple-element.85), channel_id=1, source_target_pairs={{0,14},{2,0},{4,2},{6,4},{8,6},{10,8},{12,10},{14,12},{1,15},{3,1}... | collective-permute-start | bytes 417800 | tf_op jit(solution)/shard_map/ppermute | solution.py:22
  88.0 6.6 %collective-permute-start.15 = (f32[16,2176]{1,0:T(8,128)S(1)}, f32[16,2176]{1,0:T(8,128)S(1)}, u32[]{:S(2)}, u32[]{:S(2)}) collective-permute-start(f32[16,2176]{1,0:T(8,128)S(1)} %get-tuple-element.79), channel_id=1, source_target_pairs={{0,2},{2,4},{4,6},{6,8},{8,10},{10,12},{12,14},{14,0},{1,3},{3,5},... | collective-permute-start | bytes 417800 | tf_op jit(solution)/shard_map/ppermute | solution.py:22
  88.9 7.0 %collective-permute-start.26 = (f32[16,2176]{1,0:T(8,128)S(1)}, f32[16,2176]{1,0:T(8,128)S(1)}, u32[]{:S(2)}, u32[]{:S(2)}) collective-permute-start(f32[16,2176]{1,0:T(8,128)S(1)} %get-tuple-element.99), channel_id=1, source_target_pairs={{0,2},{2,4},{4,6},{6,8},{8,10},{10,12},{12,14},{14,0},{1,3},{3,5},... | collective-permute-start | bytes 417800 | tf_op jit(solution)/shard_map/ppermute | solution.py:22
  89.4 6.6 %collective-permute-start.30 = (f32[16,2176]{1,0:T(8,128)S(1)}, f32[16,2176]{1,0:T(8,128)S(1)}, u32[]{:S(2)}, u32[]{:S(2)}) collective-permute-start(f32[16,2176]{1,0:T(8,128)S(1)} %get-tuple-element.109), channel_id=1, source_target_pairs={{0,14},{2,0},{4,2},{6,4},{8,6},{10,8},{12,10},{14,12},{1,15},{3,1}... | collective-permute-start | bytes 417800 | tf_op jit(solution)/shard_map/ppermute | solution.py:22
  93.2 5.1 %collective-permute-start.19 = (f32[16,2176]{1,0:T(8,128)S(1)}, f32[16,2176]{1,0:T(8,128)S(1)}, u32[]{:S(2)}, u32[]{:S(2)}) collective-permute-start(f32[16,2176]{1,0:T(8,128)S(1)} %get-tuple-element.87), channel_id=1, source_target_pairs={{0,14},{2,0},{4,2},{6,4},{8,6},{10,8},{12,10},{14,12},{1,15},{3,1}... | collective-permute-start | bytes 417800 | tf_op jit(solution)/shard_map/ppermute | solution.py:22
  94.7 6.3 %collective-permute-start.16 = (f32[16,2176]{1,0:T(8,128)S(1)}, f32[16,2176]{1,0:T(8,128)S(1)}, u32[]{:S(2)}, u32[]{:S(2)}) collective-permute-start(f32[16,2176]{1,0:T(8,128)S(1)} %get-tuple-element.81), channel_id=1, source_target_pairs={{0,2},{2,4},{4,6},{6,8},{8,10},{10,12},{12,14},{14,0},{1,3},{3,5},... | collective-permute-start | bytes 417800 | tf_op jit(solution)/shard_map/ppermute | solution.py:22
  101.1 6.6 %collective-permute-start.31 = (f32[16,2176]{1,0:T(8,128)S(1)}, f32[16,2176]{1,0:T(8,128)S(1)}, u32[]{:S(2)}, u32[]{:S(2)}) collective-permute-start(f32[16,2176]{1,0:T(8,128)S(1)} %get-tuple-element.113), channel_id=1, source_target_pairs={{0,16},{16,0},{1,17},{17,1},{2,18},{18,2},{3,19},{19,3},{4,20},{20... | collective-permute-start | bytes 417800 | tf_op jit(solution)/shard_map/ppermute | solution.py:22

commit v3 on v2

--- a/solution.py
+++ b/solution.py
@@ -134,9 +134,9 @@
     )(rest, high, low)
 
 
-def tails_of(softness, pieces, layout, both, put_stats):
+def tails_of(softness, pieces, layout, both, put_stats, at=0):
     lane = lax.broadcasted_iota(jnp.int32, (8, EXT), 1)
-    owned, at, rows = jnp.zeros((8, EXT), F32), 0, both.shape[0] // 2
+    owned, rows = jnp.zeros((8, EXT), F32), both.shape[0] // 2
     for ref, blocks in zip(pieces, layout, strict=True):
         for b, (d, e) in enumerate(blocks):
             score = ref[b * 32 : b * 32 + 32, :] * (-1.0 / softness)
@@ -165,20 +165,27 @@
     return twice[:rows] + twice[rows:] + mul(both[:rows, :], low[part, :])
 
 
-def early_kernel(softness, layout, *refs):
-    pieces, (high, low, out, both) = refs[: len(layout)], refs[len(layout) :]
-    n_inst = high.shape[0]
-
-    def put_stats(row, stats):
-        out[row : row + 8, n_inst:] = stats
-
-    owned = tails_of(softness, pieces, layout, both, put_stats)
+def early_kernel(softness, layouts, *refs):
+    n = len(layouts)
+    pieces, (high, low), outs, both = refs[:n], refs[n : n + 2], refs[n + 2 : -1], refs[-1]
+    n_inst, at, starts = high.shape[0], 0, []
     lane = lax.broadcasted_iota(jnp.int32, (8, EXT), 1)
-    out[:8, n_inst:] = jnp.where(lane < 64, out[:8, n_inst:], owned)
+    for piece, layout, out in zip(pieces, layouts, outs, strict=True):
+
+        def put_stats(row, stats, out=out, at=at):
+            out[row - at : row - at + 8, n_inst:] = stats
+
+        owned = tails_of(softness, [piece], [layout], both, put_stats, at)
+        out[:8, n_inst:] = jnp.where(lane < 64, out[:8, n_inst:], owned)
+        starts.append(at)
+        at += piece.shape[0]
 
     @pl.loop(0, n_inst // SB)
     def _(i):
-        out[:, pl.ds(pl.multiple_of(i * SB, SB), SB)] = block_product(both, high, low, i)
+        acc = block_product(both, high, low, i)
+        cols = pl.ds(pl.multiple_of(i * SB, SB), SB)
+        for first, out in zip(starts, outs, strict=True):
+            out[:, cols] = acc[first : first + out.shape[0]]
 
 
 def late_kernel(softness, layout, done_layout, *refs):
@@ -358,10 +365,9 @@
         ((row,), [[(d, 0) for d in range(Y)]], (rest,), [[(d, 1) for d in range(Y)]]),
         ((both,), [[(0, 0), (0, 1)]], (e1, e2, e3), [[(d, 0), (d, 1)] for d in (1, 2, 3)]),
     )
-    dones = []
-    for pieces, layout, _, _ in groups:
-        kernel = functools.partial(early_kernel, softness, layout)
-        dones += gradients(kernel, pieces, high, low, [pieces[0].shape[0]], [])
+    kernel = functools.partial(early_kernel, softness, [layout[0] for _, layout, _, _ in groups])
+    early = [pieces[0] for pieces, _, _, _ in groups]
+    dones = gradients(kernel, early, high, low, [p.shape[0] for p in early], [])
     dones = lax.optimization_barrier(tuple(dones))
 
     ends = []

time: 109 us -> 109 us (level)
  waiting for transfers between devices: 31.6 us -> 34.7 us
  Pallas kernels: 29.2 us -> 26.2 us
    ppermute x32, waiting for transfers between devices: 31.6 us -> 34.7 us  [send(): return lax.ppermute(x, axis, [(i, (i + shift) % n) for i in range(n)])]
    pallas_call x4 -> x3, Pallas kernels: 16.9 us -> 13.9 us  [gradients(): pl.pallas_call(kernel, out_shape=[jax.ShapeDtypeStruct((r, n_inst + EXT),...]
  transfers between devices with their start and end apart: 32 -> 32, of which waited for: 16 -> 18; matrix products, arithmetic and copies ran while one was open for 0% -> 0% of each run, Pallas kernels for 19% -> 16%
where the time goes in v3:
time: 109 us
  starting transfers between devices  46.7 us (43%)
  waiting for transfers between devices  34.7 us (32%)
  Pallas kernels  26.2 us (24%)
    ppermute x32, starting transfers between devices, send(): return lax.ppermute(x, axis, [(i, (i + shift) % n) for i in range(n)])  46.7 us
    ppermute x32, waiting for transfers between devices, send(): return lax.ppermute(x, axis, [(i, (i + shift) % n) for i in range(n)])  34.7 us
    pallas_call x3, Pallas kernels, gradients(): pl.pallas_call(kernel, out_shape=[jax.ShapeDtypeStruct((r, n_inst + EXT),...  13.9 us
    pallas_call x1, Pallas kernels, first_profits(): pl.pallas_call(first_pnl_kernel, out_shape=[jax.ShapeDtypeStruct(*o) for...  7.4 us
    pallas_call x1, Pallas kernels, rest_profits(): pl.pallas_call(rest_pnl_kernel, out_shape=[jax.ShapeDtypeStruct((r, n), F...  2.47 us
    pallas_call x14, Pallas kernels, call(): pl.pallas_call(kernel, out_shape=[jax.ShapeDtypeStruct(s, F32) for s in o...  2.42 us
  transfers between devices with their start and end apart: 32, of which 18 were waited for; matrix products, arithmetic and copies ran while one was open for 0% of the time, Pallas kernels for 16%

profile of v3, /device:TPU:2, one launch (start us, length us, event | category | flops | bytes accessed | tf_op | source)
XLA Modules:
  0.0 108.7 jit_solution(4045008796090564777)
XLA Ops:
  0.6 7.4 %shard_map.50 = (f32[128,1024]{1,0:T(8,128)S(1)}, f32[64,1024]{1,0:T(8,128)S(1)}, f32[64,1024]{1,0:T(8,128)S(1)}, f32[64,1024]{1,0:T(8,128)S(1)}, bf16[2048,1024...) custom-call(s32[512,2048]{1,0:T(8,128)} %pos.1, s32[8,16]{1,0:T(8,128)} %grid_in.1, ...), custom_call_target="tpu_custom_call" | custom-call | flops 2684354560 | bytes 12582912 | tf_op jit(solution)/shard_map/pallas_call | solution.py:96
  8.0 2.3 %collective-permute-start = (f32[128,1024]{1,0:T(8,128)S(1)}, f32[128,1024]{1,0:T(8,128)S(1)}, u32[]{:S(2)}, u32[]{:S(2)}) collective-permute-start(f32[128,1024]{1,0:T(8,128)S(1)} %get-tuple-element.63), channel_id=1, source_target_pairs={{0,32},{32,0},{1,33},{33,1},{2,34},{34,2},{3,35},{35,3},{4,36},{36... | collective-permute-start | bytes 1572872 | tf_op jit(solution)/shard_map/ppermute | solution.py:22
  10.4 1.5 %collective-permute-start.10 = (f32[64,1024]{1,0:T(8,128)S(1)}, f32[64,1024]{1,0:T(8,128)S(1)}, u32[]{:S(2)}, u32[]{:S(2)}) collective-permute-start(f32[64,1024]{1,0:T(8,128)S(1)} %get-tuple-element.67), channel_id=1, source_target_pairs={{0,128},{64,192},{128,0},{192,64},{1,129},{65,193},{129,1},{193,65... | collective-permute-start | bytes 786440 | tf_op jit(solution)/shard_map/ppermute | solution.py:22
  11.8 1.1 collective-permute-start.9
  12.9 1.0 collective-permute-start.8
  13.9 2.5 %shard_map.51 = (f32[128,1024]{1,0:T(8,128)S(1)}, f32[64,1024]{1,0:T(8,128)S(1)}) custom-call(bf16[192,2048]{1,0:T(8,128)(2,1)S(1)} %get-tuple-element.59.rest, bf16[2048,1024]{1,0:T(8,128)(2,1)S(1)} %get-tuple-element.60.high.refs_2_.refs_4_, bf16[2048,1024]{1,0:T(8,128)(2,1)S(1)} %get-tuple-element.61.low.refs_3_.refs_5_), custom_call_target="tpu_custom_call" | custom-call | flops 1610612736 | bytes 12582912 | tf_op jit(solution)/shard_map/pallas_call | solution.py:127
  16.4 5.5 %collective-permute-done = f32[128,1024]{1,0:T(8,128)S(1)} collective-permute-done((f32[128,1024]{1,0:T(8,128)S(1)}, f32[128,1024]{1,0:T(8,128)S(1)}, u32[]{:S(2)}, u32[]{:S(2)}) %collective-permute-start) | collective-permute-done | bytes 524320 | tf_op jit(solution)/shard_map/ppermute | solution.py:22
  21.9 3.3 %collective-permute-start.3 = (f32[32,1024]{1,0:T(8,128)S(1)}, f32[32,1024]{1,0:T(8,128)S(1)}, u32[]{:S(2)}, u32[]{:S(2)}) collective-permute-start(f32[32,1024]{1,0:T(8,128)S(1)} %get-tuple-element.117), channel_id=1, source_target_pairs={{0,128},{64,192},{128,0},{192,64},{1,129},{65,193},{129,1},{193,65... | collective-permute-start | bytes 393224 | tf_op jit(solution)/shard_map/ppermute | solution.py:22
  25.1 1.1 collective-permute-start.2
  26.2 1.0 collective-permute-start.1
  27.2 0.6 collective-permute-start.11
  27.9 1.9 %collective-permute-done.3 = f32[32,1024]{1,0:T(8,128)S(1)} collective-permute-done((f32[32,1024]{1,0:T(8,128)S(1)}, f32[32,1024]{1,0:T(8,128)S(1)}, u32[]{:S(2)}, u32[]{:S(2)}) %collective-permute-start.3) | collective-permute-done | bytes 131104 | tf_op jit(solution)/shard_map/ppermute | solution.py:22
  29.7 1.2 %collective-permute-done.2 = f32[32,1024]{1,0:T(8,128)S(1)} collective-permute-done((f32[32,1024]{1,0:T(8,128)S(1)}, f32[32,1024]{1,0:T(8,128)S(1)}, u32[]{:S(2)}, u32[]{:S(2)}) %collective-permute-start.2) | collective-permute-done | bytes 131104 | tf_op jit(solution)/shard_map/ppermute | solution.py:22
  30.9 1.4 %collective-permute-done.1 = f32[32,1024]{1,0:T(8,128)S(1)} collective-permute-done((f32[32,1024]{1,0:T(8,128)S(1)}, f32[32,1024]{1,0:T(8,128)S(1)}, u32[]{:S(2)}, u32[]{:S(2)}) %collective-permute-start.1) | collective-permute-done | bytes 131104 | tf_op jit(solution)/shard_map/ppermute | solution.py:22
  32.5 2.7 %collective-permute-start.5 = (f32[32,1024]{1,0:T(8,128)S(1)}, f32[32,1024]{1,0:T(8,128)S(1)}, u32[]{:S(2)}, u32[]{:S(2)}) collective-permute-start(f32[32,1024]{1,0:T(8,128)S(1)} %fusion.2), channel_id=1, source_target_pairs={{0,128},{64,192},{128,0},{192,64},{1,129},{65,193},{129,1},{193,65... | collective-permute-start | bytes 393224 | tf_op jit(solution)/shard_map/ppermute | solution.py:22
  35.2 1.3 %collective-permute-start.4 = (f32[32,1024]{1,0:T(8,128)S(1)}, f32[32,1024]{1,0:T(8,128)S(1)}, u32[]{:S(2)}, u32[]{:S(2)}) collective-permute-start(f32[32,1024]{1,0:T(8,128)S(1)} %fusion.2), channel_id=1, source_target_pairs={{0,192},{64,0},{128,64},{192,128},{1,193},{65,1},{129,65},{193,129... | collective-permute-start | bytes 393224 | tf_op jit(solution)/shard_map/ppermute | solution.py:22
  36.6 4.1 %collective-permute-done.6 = f32[32,1024]{1,0:T(8,128)S(1)} collective-permute-done((f32[32,1024]{1,0:T(8,128)S(1)}, f32[32,1024]{1,0:T(8,128)S(1)}, u32[]{:S(2)}, u32[]{:S(2)}) %collective-permute-start.6) | collective-permute-done | bytes 131104 | tf_op jit(solution)/shard_map/ppermute | solution.py:22
  40.7 0.2 collective-permute-done.4
  41.0 0.6 collective-permute-start.7
  41.6 2.8 %collective-permute-start.20 = (f32[64,1024]{1,0:T(8,128)S(1)}, f32[64,1024]{1,0:T(8,128)S(1)}, u32[]{:S(2)}, u32[]{:S(2)}) collective-permute-start(f32[64,1024]{1,0:T(8,128)S(1)} %maximum_add_fusion.refs_1_), channel_id=1, source_target_pairs={{0,192},{64,0},{128,64},{192,128},{1,193},{65,1},{129,65},{193,129... | collective-permute-start | bytes 786440 | tf_op jit(solution)/shard_map/ppermute | solution.py:22
  44.4 0.8 collective-permute-start.21
  45.1 0.2 collective-permute-start.22
  45.3 4.7 %shard_map.52 = (f32[128,2176]{1,0:T(8,128)S(1)}, f32[64,2176]{1,0:T(8,128)S(1)}) custom-call(f32[128,1024]{1,0:T(8,128)S(1)} %pad_maximum_fusion.refs_0_, f32[64,1024]{1,0:T(8,128)S(1)} %maximum_add_fusion.refs_1_, bf16[2048,1024]{1,0:T(8,128)(2,1)S(1)} %get-tuple-element.60.high.refs_2_.refs_4_, bf16[2048,1024]{1,0:T(8,128)(2,1)S(1)} %get-tuple-element.61.low.refs_3_.refs_5_), custom_call_target="tpu_custom_call" | custom-call | flops 2415919104 | bytes 8388608 | tf_op jit(solution)/shard_map/pallas_call | solution.py:236
  50.0 2.3 %collective-permute-done.20.refs_0_ = f32[64,1024]{1,0:T(8,128)S(1)} collective-permute-done((f32[64,1024]{1,0:T(8,128)S(1)}, f32[64,1024]{1,0:T(8,128)S(1)}, u32[]{:S(2)}, u32[]{:S(2)}) %collective-permute-start.20) | collective-permute-done | bytes 262176 | tf_op jit(solution)/shard_map/ppermute | solution.py:22
  52.4 0.5 collective-permute-done.21.refs_1_
  52.8 2.7 %collective-permute-done.22.refs_2_ = f32[64,1024]{1,0:T(8,128)S(1)} collective-permute-done((f32[64,1024]{1,0:T(8,128)S(1)}, f32[64,1024]{1,0:T(8,128)S(1)}, u32[]{:S(2)}, u32[]{:S(2)}) %collective-permute-start.22) | collective-permute-done | bytes 262176 | tf_op jit(solution)/shard_map/ppermute | solution.py:22
  55.5 5.0 %shard_map.60 = (f32[128,2176]{1,0:T(8,128)S(1)}, f32[128,2176]{1,0:T(8,128)S(1)}) custom-call(f32[64,1024]{1,0:T(8,128)S(1)} %collective-permute-done.20.refs_0_, f32[64,1024]{1,0:T(8,128)S(1)} %collective-permute-done.21.refs_1_, f32[64,1024]{1,0:T(8,128)S(1)} %collective-permute-done.22.refs_2_, f32[64,2176]{1,0:T(8,128)S(1)} %get-tuple-element.90.refs_3_, ...), custom_call_target="tpu_custom_call" | custom-call | flops 2415919104 | bytes 8388608 | tf_op jit(solution)/shard_map/pallas_call | solution.py:236
  60.5 0.1 collective-permute-start.23
  60.6 4.2 %shard_map.53 = (f32[128,2176]{1,0:T(8,128)S(1)}, f32[128,2176]{1,0:T(8,128)S(1)}) custom-call(f32[128,1024]{1,0:T(8,128)S(1)} %collective-permute-done.7.refs_0_, f32[128,2176]{1,0:T(8,128)S(1)} %get-tuple-element.68.refs_1_, bf16[2048,1024]{1,0:T(8,128)(2,1)S(1)} %get-tuple-element.60.high.refs_2_.refs_4_, ...), custom_call_target="tpu_custom_call" | custom-call | flops 1610612736 | bytes 8388608 | tf_op jit(solution)/shard_map/pallas_call | solution.py:236
  64.8 0.6 collective-permute-start.12
  65.4 0.2 shard_map.61
  65.6 6.0 %collective-permute-start.27 = (f32[16,2176]{1,0:T(8,128)S(1)}, f32[16,2176]{1,0:T(8,128)S(1)}, u32[]{:S(2)}, u32[]{:S(2)}) collective-permute-start(f32[16,2176]{1,0:T(8,128)S(1)} %get-tuple-element.103), channel_id=1, source_target_pairs={{0,14},{2,0},{4,2},{6,4},{8,6},{10,8},{12,10},{14,12},{1,15},{3,1}... | collective-permute-start | bytes 417800 | tf_op jit(solution)/shard_map/ppermute | solution.py:22
  71.7 0.2 shard_map.54
  72.1 2.7 %collective-permute-done.27.came = f32[16,2176]{1,0:T(8,128)S(1)} collective-permute-done((f32[16,2176]{1,0:T(8,128)S(1)}, f32[16,2176]{1,0:T(8,128)S(1)}, u32[]{:S(2)}, u32[]{:S(2)}) %collective-permute-start.27) | collective-permute-done | bytes 139296 | tf_op jit(solution)/shard_map/ppermute | solution.py:22
  74.8 0.1 shard_map.64
  74.9 3.8 %collective-permute-start.28 = (f32[16,2176]{1,0:T(8,128)S(1)}, f32[16,2176]{1,0:T(8,128)S(1)}, u32[]{:S(2)}, u32[]{:S(2)}) collective-permute-start(f32[16,2176]{1,0:T(8,128)S(1)} %get-tuple-element.105), channel_id=1, source_target_pairs={{0,14},{2,0},{4,2},{6,4},{8,6},{10,8},{12,10},{14,12},{1,15},{3,1}... | collective-permute-start | bytes 417800 | tf_op jit(solution)/shard_map/ppermute | solution.py:22
  78.8 1.0 collective-permute-done.13.came
  79.7 0.1 shard_map.55
  79.8 1.0 collective-permute-start.14
  80.9 0.6 collective-permute-done.24.came
  81.5 0.1 shard_map.62
  81.7 0.7 collective-permute-done.28.came
  82.4 0.1 shard_map.65
  82.5 3.8 %collective-permute-start.29 = (f32[16,2176]{1,0:T(8,128)S(1)}, f32[16,2176]{1,0:T(8,128)S(1)}, u32[]{:S(2)}, u32[]{:S(2)}) collective-permute-start(f32[16,2176]{1,0:T(8,128)S(1)} %get-tuple-element.107), channel_id=1, source_target_pairs={{0,14},{2,0},{4,2},{6,4},{8,6},{10,8},{12,10},{14,12},{1,15},{3,1}... | collective-permute-start | bytes 417800 | tf_op jit(solution)/shard_map/ppermute | solution.py:22
  86.3 0.1 shard_map.58
  86.4 1.5 %collective-permute-start.18 = (f32[16,2176]{1,0:T(8,128)S(1)}, f32[16,2176]{1,0:T(8,128)S(1)}, u32[]{:S(2)}, u32[]{:S(2)}) collective-permute-start(f32[16,2176]{1,0:T(8,128)S(1)} %get-tuple-element.85), channel_id=1, source_target_pairs={{0,14},{2,0},{4,2},{6,4},{8,6},{10,8},{12,10},{14,12},{1,15},{3,1}... | collective-permute-start | bytes 417800 | tf_op jit(solution)/shard_map/ppermute | solution.py:22
  87.9 0.1 shard_map.56
  88.0 0.7 collective-permute-start.15
  88.7 0.2 collective-permute-done.25.came
  88.8 0.1 shard_map.63
  88.9 0.3 collective-permute-start.26
  89.3 0.1 shard_map.66
  89.4 3.7 %collective-permute-start.30 = (f32[16,2176]{1,0:T(8,128)S(1)}, f32[16,2176]{1,0:T(8,128)S(1)}, u32[]{:S(2)}, u32[]{:S(2)}) collective-permute-start(f32[16,2176]{1,0:T(8,128)S(1)} %get-tuple-element.109), channel_id=1, source_target_pairs={{0,14},{2,0},{4,2},{6,4},{8,6},{10,8},{12,10},{14,12},{1,15},{3,1}... | collective-permute-start | bytes 417800 | tf_op jit(solution)/shard_map/ppermute | solution.py:22
  93.1 0.1 shard_map.59
  93.2 1.4 %collective-permute-start.19 = (f32[16,2176]{1,0:T(8,128)S(1)}, f32[16,2176]{1,0:T(8,128)S(1)}, u32[]{:S(2)}, u32[]{:S(2)}) collective-permute-start(f32[16,2176]{1,0:T(8,128)S(1)} %get-tuple-element.87), channel_id=1, source_target_pairs={{0,14},{2,0},{4,2},{6,4},{8,6},{10,8},{12,10},{14,12},{1,15},{3,1}... | collective-permute-start | bytes 417800 | tf_op jit(solution)/shard_map/ppermute | solution.py:22
  94.6 0.1 shard_map.57
  94.7 0.8 collective-permute-start.16
  95.4 0.5 collective-permute-done.26.refs_6_
  95.9 2.4 %collective-permute-done.19.refs_2_ = f32[16,2176]{1,0:T(8,128)S(1)} collective-permute-done((f32[16,2176]{1,0:T(8,128)S(1)}, f32[16,2176]{1,0:T(8,128)S(1)}, u32[]{:S(2)}, u32[]{:S(2)}) %collective-permute-start.19) | collective-permute-done | bytes 139296 | tf_op jit(solution)/shard_map/ppermute | solution.py:22
  98.3 2.7 %collective-permute-done.16.refs_1_ = f32[16,2176]{1,0:T(8,128)S(1)} collective-permute-done((f32[16,2176]{1,0:T(8,128)S(1)}, f32[16,2176]{1,0:T(8,128)S(1)}, u32[]{:S(2)}, u32[]{:S(2)}) %collective-permute-start.16) | collective-permute-done | bytes 139296 | tf_op jit(solution)/shard_map/ppermute | solution.py:22
  101.0 0.1 shard_map.67
  101.1 2.5 %collective-permute-start.31 = (f32[16,2176]{1,0:T(8,128)S(1)}, f32[16,2176]{1,0:T(8,128)S(1)}, u32[]{:S(2)}, u32[]{:S(2)}) collective-permute-start(f32[16,2176]{1,0:T(8,128)S(1)} %get-tuple-element.113), channel_id=1, source_target_pairs={{0,16},{16,0},{1,17},{17,1},{2,18},{18,2},{3,19},{19,3},{4,20},{20... | collective-permute-start | bytes 417800 | tf_op jit(solution)/shard_map/ppermute | solution.py:22
  103.7 4.1 %collective-permute-done.31.came = f32[16,2176]{1,0:T(8,128)S(1)} collective-permute-done((f32[16,2176]{1,0:T(8,128)S(1)}, f32[16,2176]{1,0:T(8,128)S(1)}, u32[]{:S(2)}, u32[]{:S(2)}) %collective-permute-start.31) | collective-permute-done | bytes 139296 | tf_op jit(solution)/shard_map/ppermute | solution.py:22
  107.8 0.9 shard_map.68
  (25 shorter events, 0.7 us)
Async XLA Ops:
  8.0 13.8 %collective-permute-start = (f32[128,1024]{1,0:T(8,128)S(1)}, f32[128,1024]{1,0:T(8,128)S(1)}, u32[]{:S(2)}, u32[]{:S(2)}) collective-permute-start(f32[128,1024]{1,0:T(8,128)S(1)} %get-tuple-element.63), channel_id=1, source_target_pairs={{0,32},{32,0},{1,33},{33,1},{2,34},{34,2},{3,35},{35,3},{4,36},{36... | collective-permute-start | bytes 1572872 | tf_op jit(solution)/shard_map/ppermute | solution.py:22
  10.4 15.8 %collective-permute-start.10 = (f32[64,1024]{1,0:T(8,128)S(1)}, f32[64,1024]{1,0:T(8,128)S(1)}, u32[]{:S(2)}, u32[]{:S(2)}) collective-permute-start(f32[64,1024]{1,0:T(8,128)S(1)} %get-tuple-element.67), channel_id=1, source_target_pairs={{0,128},{64,192},{128,0},{192,64},{1,129},{65,193},{129,1},{193,65... | collective-permute-start | bytes 786440 | tf_op jit(solution)/shard_map/ppermute | solution.py:22
  11.8 15.3 %collective-permute-start.9 = (f32[64,1024]{1,0:T(8,128)S(1)}, f32[64,1024]{1,0:T(8,128)S(1)}, u32[]{:S(2)}, u32[]{:S(2)}) collective-permute-start(f32[64,1024]{1,0:T(8,128)S(1)} %get-tuple-element.66), channel_id=1, source_target_pairs={{0,192},{64,0},{128,64},{192,128},{1,193},{65,1},{129,65},{193,129... | collective-permute-start | bytes 786440 | tf_op jit(solution)/shard_map/ppermute | solution.py:22
  12.9 14.2 %collective-permute-start.8 = (f32[64,1024]{1,0:T(8,128)S(1)}, f32[64,1024]{1,0:T(8,128)S(1)}, u32[]{:S(2)}, u32[]{:S(2)}) collective-permute-start(f32[64,1024]{1,0:T(8,128)S(1)} %get-tuple-element.65), channel_id=1, source_target_pairs={{0,64},{64,128},{128,192},{192,0},{1,65},{65,129},{129,193},{193,1... | collective-permute-start | bytes 786440 | tf_op jit(solution)/shard_map/ppermute | solution.py:22
  21.9 7.9 %collective-permute-start.3 = (f32[32,1024]{1,0:T(8,128)S(1)}, f32[32,1024]{1,0:T(8,128)S(1)}, u32[]{:S(2)}, u32[]{:S(2)}) collective-permute-start(f32[32,1024]{1,0:T(8,128)S(1)} %get-tuple-element.117), channel_id=1, source_target_pairs={{0,128},{64,192},{128,0},{192,64},{1,129},{65,193},{129,1},{193,65... | collective-permute-start | bytes 393224 | tf_op jit(solution)/shard_map/ppermute | solution.py:22
  25.1 5.8 %collective-permute-start.2 = (f32[32,1024]{1,0:T(8,128)S(1)}, f32[32,1024]{1,0:T(8,128)S(1)}, u32[]{:S(2)}, u32[]{:S(2)}) collective-permute-start(f32[32,1024]{1,0:T(8,128)S(1)} %get-tuple-element.118), channel_id=1, source_target_pairs={{0,192},{64,0},{128,64},{192,128},{1,193},{65,1},{129,65},{193,129... | collective-permute-start | bytes 393224 | tf_op jit(solution)/shard_map/ppermute | solution.py:22
  26.2 6.2 %collective-permute-start.1 = (f32[32,1024]{1,0:T(8,128)S(1)}, f32[32,1024]{1,0:T(8,128)S(1)}, u32[]{:S(2)}, u32[]{:S(2)}) collective-permute-start(f32[32,1024]{1,0:T(8,128)S(1)} %get-tuple-element.116), channel_id=1, source_target_pairs={{0,64},{64,128},{128,192},{192,0},{1,65},{65,129},{129,193},{193,1... | collective-permute-start | bytes 393224 | tf_op jit(solution)/shard_map/ppermute | solution.py:22
  27.2 9.3 %collective-permute-start.11 = (f32[64,1024]{1,0:T(8,128)S(1)}, f32[64,1024]{1,0:T(8,128)S(1)}, u32[]{:S(2)}, u32[]{:S(2)}) collective-permute-start(f32[64,1024]{1,0:T(8,128)S(1)} %add_add_fusion), channel_id=1, source_target_pairs={{0,32},{32,0},{1,33},{33,1},{2,34},{34,2},{3,35},{35,3},{4,36},{36... | collective-permute-start | bytes 786440 | tf_op jit(solution)/shard_map/ppermute | solution.py:22
  32.4 8.3 %collective-permute-start.6 = (f32[32,1024]{1,0:T(8,128)S(1)}, f32[32,1024]{1,0:T(8,128)S(1)}, u32[]{:S(2)}, u32[]{:S(2)}) collective-permute-start(f32[32,1024]{1,0:T(8,128)S(1)} %fusion.2), channel_id=1, source_target_pairs={{0,64},{64,128},{128,192},{192,0},{1,65},{65,129},{129,193},{193,1... | collective-permute-start | bytes 393224 | tf_op jit(solution)/shard_map/ppermute | solution.py:22
  32.5 8.2 %collective-permute-start.5 = (f32[32,1024]{1,0:T(8,128)S(1)}, f32[32,1024]{1,0:T(8,128)S(1)}, u32[]{:S(2)}, u32[]{:S(2)}) collective-permute-start(f32[32,1024]{1,0:T(8,128)S(1)} %fusion.2), channel_id=1, source_target_pairs={{0,128},{64,192},{128,0},{192,64},{1,129},{65,193},{129,1},{193,65... | collective-permute-start | bytes 393224 | tf_op jit(solution)/shard_map/ppermute | solution.py:22
  35.2 5.7 %collective-permute-start.4 = (f32[32,1024]{1,0:T(8,128)S(1)}, f32[32,1024]{1,0:T(8,128)S(1)}, u32[]{:S(2)}, u32[]{:S(2)}) collective-permute-start(f32[32,1024]{1,0:T(8,128)S(1)} %fusion.2), channel_id=1, source_target_pairs={{0,192},{64,0},{128,64},{192,128},{1,193},{65,1},{129,65},{193,129... | collective-permute-start | bytes 393224 | tf_op jit(solution)/shard_map/ppermute | solution.py:22
  41.0 19.6 %collective-permute-start.7 = (f32[128,1024]{1,0:T(8,128)S(1)}, f32[128,1024]{1,0:T(8,128)S(1)}, u32[]{:S(2)}, u32[]{:S(2)}) collective-permute-start(f32[128,1024]{1,0:T(8,128)S(1)} %pad_maximum_fusion.refs_0_), channel_id=1, source_target_pairs={{0,32},{32,0},{1,33},{33,1},{2,34},{34,2},{3,35},{35,3},{4,36},{36... | collective-permute-start | bytes 1572872 | tf_op jit(solution)/shard_map/ppermute | solution.py:22
  41.6 10.7 %collective-permute-start.20 = (f32[64,1024]{1,0:T(8,128)S(1)}, f32[64,1024]{1,0:T(8,128)S(1)}, u32[]{:S(2)}, u32[]{:S(2)}) collective-permute-start(f32[64,1024]{1,0:T(8,128)S(1)} %maximum_add_fusion.refs_1_), channel_id=1, source_target_pairs={{0,192},{64,0},{128,64},{192,128},{1,193},{65,1},{129,65},{193,129... | collective-permute-start | bytes 786440 | tf_op jit(solution)/shard_map/ppermute | solution.py:22
  44.4 8.5 %collective-permute-start.21 = (f32[64,1024]{1,0:T(8,128)S(1)}, f32[64,1024]{1,0:T(8,128)S(1)}, u32[]{:S(2)}, u32[]{:S(2)}) collective-permute-start(f32[64,1024]{1,0:T(8,128)S(1)} %maximum_add_fusion.refs_1_), channel_id=1, source_target_pairs={{0,128},{64,192},{128,0},{192,64},{1,129},{65,193},{129,1},{193,65... | collective-permute-start | bytes 786440 | tf_op jit(solution)/shard_map/ppermute | solution.py:22
  45.1 10.4 %collective-permute-start.22 = (f32[64,1024]{1,0:T(8,128)S(1)}, f32[64,1024]{1,0:T(8,128)S(1)}, u32[]{:S(2)}, u32[]{:S(2)}) collective-permute-start(f32[64,1024]{1,0:T(8,128)S(1)} %maximum_add_fusion.refs_1_), channel_id=1, source_target_pairs={{0,64},{64,128},{128,192},{192,0},{1,65},{65,129},{129,193},{193,1... | collective-permute-start | bytes 786440 | tf_op jit(solution)/shard_map/ppermute | solution.py:22
  60.5 4.9 %collective-permute-start.23 = (f32[128,2176]{1,0:T(8,128)S(1)}, f32[128,2176]{1,0:T(8,128)S(1)}, u32[]{:S(2)}, u32[]{:S(2)}) collective-permute-start(f32[128,2176]{1,0:T(8,128)S(1)} %get-tuple-element.92), channel_id=1, source_target_pairs={{0,1},{1,0},{2,3},{3,2},{4,5},{5,4},{6,7},{7,6},{8,9},{9,8},{10,11... | collective-permute-start | bytes 3342344 | tf_op jit(solution)/shard_map/ppermute | solution.py:22
  64.8 6.9 %collective-permute-start.12 = (f32[128,2176]{1,0:T(8,128)S(1)}, f32[128,2176]{1,0:T(8,128)S(1)}, u32[]{:S(2)}, u32[]{:S(2)}) collective-permute-start(f32[128,2176]{1,0:T(8,128)S(1)} %get-tuple-element.70), channel_id=1, source_target_pairs={{0,1},{1,0},{2,3},{3,2},{4,5},{5,4},{6,7},{7,6},{8,9},{9,8},{10,11... | collective-permute-start | bytes 3342344 | tf_op jit(solution)/shard_map/ppermute | solution.py:22
  65.6 9.2 %collective-permute-start.27 = (f32[16,2176]{1,0:T(8,128)S(1)}, f32[16,2176]{1,0:T(8,128)S(1)}, u32[]{:S(2)}, u32[]{:S(2)}) collective-permute-start(f32[16,2176]{1,0:T(8,128)S(1)} %get-tuple-element.103), channel_id=1, source_target_pairs={{0,14},{2,0},{4,2},{6,4},{8,6},{10,8},{12,10},{14,12},{1,15},{3,1}... | collective-permute-start | bytes 417800 | tf_op jit(solution)/shard_map/ppermute | solution.py:22
  71.9 7.8 %collective-permute-start.13 = (f32[16,2176]{1,0:T(8,128)S(1)}, f32[16,2176]{1,0:T(8,128)S(1)}, u32[]{:S(2)}, u32[]{:S(2)}) collective-permute-start(f32[16,2176]{1,0:T(8,128)S(1)} %get-tuple-element.75), channel_id=1, source_target_pairs={{0,2},{2,4},{4,6},{6,8},{8,10},{10,12},{12,14},{14,0},{1,3},{3,5},... | collective-permute-start | bytes 417800 | tf_op jit(solution)/shard_map/ppermute | solution.py:22
  72.0 9.5 %collective-permute-start.24 = (f32[16,2176]{1,0:T(8,128)S(1)}, f32[16,2176]{1,0:T(8,128)S(1)}, u32[]{:S(2)}, u32[]{:S(2)}) collective-permute-start(f32[16,2176]{1,0:T(8,128)S(1)} %get-tuple-element.96), channel_id=1, source_target_pairs={{0,2},{2,4},{4,6},{6,8},{8,10},{10,12},{12,14},{14,0},{1,3},{3,5},... | collective-permute-start | bytes 417800 | tf_op jit(solution)/shard_map/ppermute | solution.py:22
  74.9 7.5 %collective-permute-start.28 = (f32[16,2176]{1,0:T(8,128)S(1)}, f32[16,2176]{1,0:T(8,128)S(1)}, u32[]{:S(2)}, u32[]{:S(2)}) collective-permute-start(f32[16,2176]{1,0:T(8,128)S(1)} %get-tuple-element.105), channel_id=1, source_target_pairs={{0,14},{2,0},{4,2},{6,4},{8,6},{10,8},{12,10},{14,12},{1,15},{3,1}... | collective-permute-start | bytes 417800 | tf_op jit(solution)/shard_map/ppermute | solution.py:22
  78.7 7.6 %collective-permute-start.17 = (f32[16,2176]{1,0:T(8,128)S(1)}, f32[16,2176]{1,0:T(8,128)S(1)}, u32[]{:S(2)}, u32[]{:S(2)}) collective-permute-start(f32[16,2176]{1,0:T(8,128)S(1)} %get-tuple-element.84), channel_id=1, source_target_pairs={{0,14},{2,0},{4,2},{6,4},{8,6},{10,8},{12,10},{14,12},{1,15},{3,1}... | collective-permute-start | bytes 417800 | tf_op jit(solution)/shard_map/ppermute | solution.py:22
  79.8 8.0 %collective-permute-start.14 = (f32[16,2176]{1,0:T(8,128)S(1)}, f32[16,2176]{1,0:T(8,128)S(1)}, u32[]{:S(2)}, u32[]{:S(2)}) collective-permute-start(f32[16,2176]{1,0:T(8,128)S(1)} %get-tuple-element.77), channel_id=1, source_target_pairs={{0,2},{2,4},{4,6},{6,8},{8,10},{10,12},{12,14},{14,0},{1,3},{3,5},... | collective-permute-start | bytes 417800 | tf_op jit(solution)/shard_map/ppermute | solution.py:22
  81.6 7.2 %collective-permute-start.25 = (f32[16,2176]{1,0:T(8,128)S(1)}, f32[16,2176]{1,0:T(8,128)S(1)}, u32[]{:S(2)}, u32[]{:S(2)}) collective-permute-start(f32[16,2176]{1,0:T(8,128)S(1)} %get-tuple-element.97), channel_id=1, source_target_pairs={{0,2},{2,4},{4,6},{6,8},{8,10},{10,12},{12,14},{14,0},{1,3},{3,5},... | collective-permute-start | bytes 417800 | tf_op jit(solution)/shard_map/ppermute | solution.py:22
  82.5 6.7 %collective-permute-start.29 = (f32[16,2176]{1,0:T(8,128)S(1)}, f32[16,2176]{1,0:T(8,128)S(1)}, u32[]{:S(2)}, u32[]{:S(2)}) collective-permute-start(f32[16,2176]{1,0:T(8,128)S(1)} %get-tuple-element.107), channel_id=1, source_target_pairs={{0,14},{2,0},{4,2},{6,4},{8,6},{10,8},{12,10},{14,12},{1,15},{3,1}... | collective-permute-start | bytes 417800 | tf_op jit(solution)/shard_map/ppermute | solution.py:22
  86.4 6.7 %collective-permute-start.18 = (f32[16,2176]{1,0:T(8,128)S(1)}, f32[16,2176]{1,0:T(8,128)S(1)}, u32[]{:S(2)}, u32[]{:S(2)}) collective-permute-start(f32[16,2176]{1,0:T(8,128)S(1)} %get-tuple-element.85), channel_id=1, source_target_pairs={{0,14},{2,0},{4,2},{6,4},{8,6},{10,8},{12,10},{14,12},{1,15},{3,1}... | collective-permute-start | bytes 417800 | tf_op jit(solution)/shard_map/ppermute | solution.py:22
  88.0 6.6 %collective-permute-start.15 = (f32[16,2176]{1,0:T(8,128)S(1)}, f32[16,2176]{1,0:T(8,128)S(1)}, u32[]{:S(2)}, u32[]{:S(2)}) collective-permute-start(f32[16,2176]{1,0:T(8,128)S(1)} %get-tuple-element.79), channel_id=1, source_target_pairs={{0,2},{2,4},{4,6},{6,8},{8,10},{10,12},{12,14},{14,0},{1,3},{3,5},... | collective-permute-start | bytes 417800 | tf_op jit(solution)/shard_map/ppermute | solution.py:22
  88.9 7.0 %collective-permute-start.26 = (f32[16,2176]{1,0:T(8,128)S(1)}, f32[16,2176]{1,0:T(8,128)S(1)}, u32[]{:S(2)}, u32[]{:S(2)}) collective-permute-start(f32[16,2176]{1,0:T(8,128)S(1)} %get-tuple-element.99), channel_id=1, source_target_pairs={{0,2},{2,4},{4,6},{6,8},{8,10},{10,12},{12,14},{14,0},{1,3},{3,5},... | collective-permute-start | bytes 417800 | tf_op jit(solution)/shard_map/ppermute | solution.py:22
  89.4 6.6 %collective-permute-start.30 = (f32[16,2176]{1,0:T(8,128)S(1)}, f32[16,2176]{1,0:T(8,128)S(1)}, u32[]{:S(2)}, u32[]{:S(2)}) collective-permute-start(f32[16,2176]{1,0:T(8,128)S(1)} %get-tuple-element.109), channel_id=1, source_target_pairs={{0,14},{2,0},{4,2},{6,4},{8,6},{10,8},{12,10},{14,12},{1,15},{3,1}... | collective-permute-start | bytes 417800 | tf_op jit(solution)/shard_map/ppermute | solution.py:22
  93.2 5.1 %collective-permute-start.19 = (f32[16,2176]{1,0:T(8,128)S(1)}, f32[16,2176]{1,0:T(8,128)S(1)}, u32[]{:S(2)}, u32[]{:S(2)}) collective-permute-start(f32[16,2176]{1,0:T(8,128)S(1)} %get-tuple-element.87), channel_id=1, source_target_pairs={{0,14},{2,0},{4,2},{6,4},{8,6},{10,8},{12,10},{14,12},{1,15},{3,1}... | collective-permute-start | bytes 417800 | tf_op jit(solution)/shard_map/ppermute | solution.py:22
  94.7 6.3 %collective-permute-start.16 = (f32[16,2176]{1,0:T(8,128)S(1)}, f32[16,2176]{1,0:T(8,128)S(1)}, u32[]{:S(2)}, u32[]{:S(2)}) collective-permute-start(f32[16,2176]{1,0:T(8,128)S(1)} %get-tuple-element.81), channel_id=1, source_target_pairs={{0,2},{2,4},{4,6},{6,8},{8,10},{10,12},{12,14},{14,0},{1,3},{3,5},... | collective-permute-start | bytes 417800 | tf_op jit(solution)/shard_map/ppermute | solution.py:22
  101.1 6.6 %collective-permute-start.31 = (f32[16,2176]{1,0:T(8,128)S(1)}, f32[16,2176]{1,0:T(8,128)S(1)}, u32[]{:S(2)}, u32[]{:S(2)}) collective-permute-start(f32[16,2176]{1,0:T(8,128)S(1)} %get-tuple-element.113), channel_id=1, source_target_pairs={{0,16},{16,0},{1,17},{17,1},{2,18},{18,2},{3,19},{19,3},{4,20},{20... | collective-permute-start | bytes 417800 | tf_op jit(solution)/shard_map/ppermute | solution.py:22
